TPU v7x, 128 devices: a whole 4x4x4 slice. The times are simulated.
128 devices in a mesh: blk: 32 (over y_hi, z, x), rep: 4 (over y_lo, core).
Axes of the slice: x: 4, y: 4 (y_hi: 2, y_lo: 2; y = y_hi * 2 + y_lo), z: 4, core: 2. Of those that a mesh axis runs over, the one named last changes fastest.
Arguments:
- image_emb: bfloat16 [16384, 1024], P(('blk', 'rep')), may hold values from -8 to 8
- curve_emb: bfloat16 [16384, 1024], P(('blk', 'rep')), may hold values from -8 to 8
Outputs:
- loss_value: float32 [], replicated
- image_grad: float32 [16384, 1024], P(('blk', 'rep'))
- curve_grad: float32 [16384, 1024], P(('blk', 'rep'))
All inputs are finite; a program needn't handle non-finite values.
Results may differ from a plain program's by a relative error of at most 0.0015.
Values may be sent and summed in bfloat16 or wider, within the bound.
A program may use at most 128 MiB of HBM per device.

v0:
```python
import math

import jax
import jax.numpy as jnp
from jax import lax
from jax.sharding import PartitionSpec as P


def merged(value, axis, combine):
    everything = jax.tree.map(lambda part: lax.all_gather(part, axis), value)
    leading = jax.tree.map(lambda part: part[0], everything)

    def lap(k, so_far):
        return combine(so_far, jax.tree.map(lambda part: part[k], everything))

    return lax.fori_loop(1, lax.axis_size(axis), lap, leading)


def combine(left_pair, right_pair):
    highest = jnp.maximum(left_pair[0], right_pair[0])
    summed = left_pair[1] * jnp.exp(left_pair[0] - highest) + right_pair[1] * jnp.exp(
        right_pair[0] - highest
    )
    return (highest, summed)


def scores_of(row_block, columns, logit_gain):
    return (
        jnp.einsum("rd,cd->rc", row_block, columns, preferred_element_type=jnp.float32) * logit_gain
    )


def shards(image_emb, curve_emb):
    local_rows, feature_count = image_emb.shape
    logit_gain = math.sqrt(feature_count)
    blk_count = lax.axis_size("blk")
    rep_count = lax.axis_size("rep")
    blk_index = lax.axis_index("blk")
    rep_index = lax.axis_index("rep")
    image_block = lax.all_gather(image_emb, "rep", axis=0, tiled=True)
    block_rows = image_block.shape[0]
    column_total = local_rows * blk_count
    group_size = 4
    tile_cols = local_rows * group_size
    tile_count = column_total // tile_cols
    row_init = (jnp.full((block_rows,), -1e30, jnp.float32), jnp.zeros((block_rows,), jnp.float32))
    positive = (
        jnp.sum(image_emb.astype(jnp.float32) * curve_emb.astype(jnp.float32), axis=1) * logit_gain
    )
    initial = (
        row_init[0],
        row_init[1],
        jnp.zeros((column_total,), jnp.float32),
        jnp.zeros((column_total,), jnp.float32),
    )
    scores = scores_of(
        image_block, lax.all_gather(curve_emb, "blk", axis=0, tiled=True), logit_gain
    )
    highest = jnp.maximum((initial[0], initial[1])[0], jnp.max(scores, axis=1))
    summed = jnp.sum(jnp.exp(scores - highest[:, None]), axis=1)
    col_high = jnp.max(scores, axis=0)
    col_sum = jnp.sum(jnp.exp(scores - col_high[None, :]), axis=0)
    row_state = (highest, summed)
    col_state = (col_high, col_sum)
    col_high = col_state[0]
    col_sum = col_state[1]
    row_high, row_sum, col_high, col_sum = (row_state[0], row_state[1], col_high, col_sum)
    curve_all = lax.all_gather(curve_emb, "blk", axis=0, tiled=True)
    row_high, row_sum = merged((row_high, row_sum), "rep", combine)
    col_high, col_sum = merged((col_high, col_sum), "blk", combine)
    row_lse = row_high + jnp.log(row_sum)
    col_lse = col_high + jnp.log(col_sum)
    own_rows = lax.dynamic_slice_in_dim(row_lse, rep_index * local_rows, local_rows, 0)
    own_cols = lax.dynamic_slice_in_dim(col_lse, blk_index * local_rows, local_rows, 0)
    partial_value = jnp.sum(own_rows - positive) + jnp.sum(own_cols - positive)

    def weights_for(columns, col_part):
        scores = scores_of(image_block, columns, logit_gain)
        return (
            (jnp.exp(scores - row_lse[:, None]) + jnp.exp(scores - col_part[None, :])) * 0.5
        ).astype(jnp.bfloat16)

    col_tiles = curve_all.reshape(tile_count, tile_cols, feature_count)
    lse_tiles = col_lse.reshape(tile_count, tile_cols)
    running_init = jnp.zeros((block_rows, feature_count), jnp.float32)

    def back_step(running, packed):
        columns, col_part = packed
        weight = weights_for(columns, col_part)
        running = running + jnp.dot(weight, columns, preferred_element_type=jnp.float32)
        contrib = (
            jnp.einsum("rc,rd->cd", weight, image_block, preferred_element_type=jnp.float32)
            * logit_gain
        )
        return (running, contrib)

    running, contribs = lax.scan(back_step, running_init, (col_tiles, lse_tiles))
    curve_part = lax.psum_scatter(
        contribs.reshape(column_total, feature_count), "blk", scatter_dimension=0, tiled=True
    )
    image_part = lax.psum_scatter(running * logit_gain, "rep", scatter_dimension=0, tiled=True)
    loss_value = lax.psum(partial_value, ("blk", "rep")) / (2.0 * column_total * rep_count)
    image_grad = image_part - logit_gain * curve_emb.astype(jnp.float32)
    curve_grad = curve_part - logit_gain * image_emb.astype(jnp.float32)
    return (loss_value, image_grad, curve_grad)


def solution(mesh):
    in_specs = (P(("blk", "rep"), None), P(("blk", "rep"), None))
    out_specs = (P(), P(("blk", "rep"), None), P(("blk", "rep"), None))
    return jax.shard_map(shards, mesh=mesh, in_specs=in_specs, out_specs=out_specs, check_vma=False)
```

profile of v0, /device:TPU:1, one launch (start us, length us, event | category | flops | bytes accessed | tf_op | source)
XLA Modules:
  0.0 772.3 jit_solution(2491032902631301436)
XLA Ops:
  8.7 25.3 %all-gather.9.cloned.1.call-done = bf16[512,1024]{1,0:T(8,128)(2,1)} async-done(((bf16[128,1024]{1,0:T(8,128)(2,1)}), bf16[512,1024]{1,0:T(8,128)(2,1)}) %all-gather.9.cloned.1.call-update) | async-done | bytes 1048592 | tf_op jit(solution)/shard_map/all_gather | solution.py:40
  34.0 107.4 %all-gather.11.cloned.1.call-done = bf16[4096,1024]{1,0:T(8,128)(2,1)} async-done(((bf16[128,1024]{1,0:T(8,128)(2,1)}), bf16[4096,1024]{1,0:T(8,128)(2,1)}) %all-gather.11.cloned.1.call-update) | async-done | bytes 8388624 | tf_op jit(solution)/shard_map/all_gather | solution.py:57
  141.4 7.4 multiply_reduce_fusion
  148.9 3.5 exponential_reduce_fusion
  152.4 6.1 all-gather.5
  158.4 5.1 all-gather.4
  163.6 79.4 %all-gather.3 = f32[131072]{0:T(1024)S(1)} all-gather(f32[4096]{0:T(1024)S(1)} %get-tuple-element.337), channel_id=5, replica_groups=mesh['blk'=32,'rep'=4] {'blk'}, dimensions={0}, use_global_device_ids=true | all-gather | bytes 540672 | tf_op jit(solution)/shard_map/all_gather | solution.py:10
  243.1 76.2 %all-gather.2 = f32[131072]{0:T(1024)S(1)} all-gather(f32[4096]{0:T(1024)S(1)} %get-tuple-element.339), channel_id=4, replica_groups=mesh['blk'=32,'rep'=4] {'blk'}, dimensions={0}, use_global_device_ids=true | all-gather | bytes 540672 | tf_op jit(solution)/shard_map/all_gather | solution.py:10
  320.4 30.5 %while.48 = (s32[]{:T(128)}, f32[4096]{0:T(1024)S(1)}, f32[4096]{0:T(1024)S(1)}, f32[32,4096]{1,0:T(8,128)}, f32[32,4096]{1,0:T(8,128)S(1)}, /*index=5*/s32[]{:T(128)}, s32[]{:T(128)}, s32[]{:T(128)}) while((s32[]{:T(128)}, f32[4096]{0:T(1024)S(1)}, f32[4096]{0:T(1024)S(1)}, f32[32,4096]{1,0:T(8,128)}, f32[32,4096]{1,0:T(8,128)S(1)}, ...), condition=%wide.region_9.0_spmd, body=%wide.region_8.0_spmd.sunk | while | flops 24581 | bytes 163971 | solution.py:16
  350.9 63.9 %while.49 = (s32[]{:T(128)}, f32[512,1024]{1,0:T(8,128)S(1)}, f32[8,512,1024]{2,1,0:T(8,128)}, bf16[8,512,1024]{2,1,0:T(8,128)(2,1)}, bf16[512,1024]{1,0:T(8,128...) while((s32[]{:T(128)}, f32[512,1024]{1,0:T(8,128)S(1)}, ...), condition=%wide.region_13.14_spmd.clone, body=%wide.region_12.13_spmd.clone.sunk | while | flops 1613758464 | bytes 12068459 | solution.py:97
  353.4 3.3 bitcast_dynamic-update-slice_fusion.2
  361.4 3.2 bitcast_dynamic-update-slice_fusion.2
  366.9 2.5 multiply_convert_fusion.2
  369.4 3.3 bitcast_dynamic-update-slice_fusion.2
  377.4 3.3 bitcast_dynamic-update-slice_fusion.2
  385.4 3.3 bitcast_dynamic-update-slice_fusion.2
  390.9 2.5 multiply_convert_fusion.2
  393.4 3.2 bitcast_dynamic-update-slice_fusion.2
  398.9 2.5 multiply_convert_fusion.2
  401.4 3.3 bitcast_dynamic-update-slice_fusion.2
  409.4 3.3 bitcast_dynamic-update-slice_fusion.2
  417.0 52.6 %reduce-scatter.3.cloned.1.call-done = f32[128,1024]{1,0:T(8,128)} async-done(((f32[512,1024]{1,0:T(8,128)}), f32[128,1024]{1,0:T(8,128)}) %reduce-scatter.3.cloned.1.call-update) | async-done | bytes 524304 | tf_op jit(solution)/shard_map/reduce_scatter | solution.py:101
  469.6 209.1 %reduce-scatter.5.cloned.1.call-done = f32[128,1024]{1,0:T(8,128)} async-done(((f32[4096,1024]{1,0:T(8,128)}), f32[128,1024]{1,0:T(8,128)}) %reduce-scatter.5.cloned.1.call-update) | async-done | bytes 524304 | tf_op jit(solution)/shard_map/reduce_scatter | solution.py:98
  683.1 80.9 %psum.7 = f32[]{:T(128)} all-reduce(f32[]{:T(128)S(6)} %add.125), channel_id=1, replica_groups=mesh['blk'=32,'rep'=4] {'blk','rep'}, use_global_device_ids=true, to_apply=%region_11.12 | all-reduce | flops 1 | bytes 8 | tf_op jit(solution)/shard_map/psum | solution.py:102
  (119 shorter events, 67.5 us)
Async XLA Ops:
  7.2 26.8 %all-gather.9.cloned.1.call-start = ((), (), s32[]{:S(2)}) async-start(), calls=%async_computation.2 | async-start | bytes 1310720 | tf_op jit(solution)/shard_map/all_gather | solution.py:40
  7.9 133.5 %all-gather.11.cloned.1.call-start = ((), (), s32[]{:S(2)}) async-start(), calls=%async_computation.3 | async-start | bytes 8650752 | tf_op jit(solution)/shard_map/all_gather | solution.py:57
  8.6 460.9 %reduce-scatter.3.cloned.1.call-start = ((), (), s32[]{:S(2)}) async-start(), calls=%async_computation.4 | async-start | bytes 2621440 | tf_op jit(solution)/shard_map/reduce_scatter | solution.py:101
  416.4 262.3 %reduce-scatter.5.cloned.1.call-start = ((), (), s32[]{:S(2)}) async-start(), calls=%async_computation.5 | async-start | bytes 17301504 | tf_op jit(solution)/shard_map/reduce_scatter | solution.py:98
  416.4 262.2 %copy-start = (bf16[128,1024]{1,0:T(8,128)(2,1)S(1)}, bf16[128,1024]{1,0:T(8,128)(2,1)}, u32[]{:S(2)}) copy-start(bf16[128,1024]{1,0:T(8,128)(2,1)} %param.8) | copy-start | bytes 786436
  416.4 262.2 %copy-start.1 = (bf16[128,1024]{1,0:T(8,128)(2,1)S(1)}, bf16[128,1024]{1,0:T(8,128)(2,1)}, u32[]{:S(2)}) copy-start(bf16[128,1024]{1,0:T(8,128)(2,1)} %param.9) | copy-start | bytes 786436
Sparse Core Ops, SparseCore 0:
  9.7 24.2 all-gather.8
  37.0 104.3 all-gather.10
  416.5 53.0 reduce-scatter.2
  472.0 206.6 reduce-scatter.4
where the time goes:
time: 774 us; the launch traced here: 772 us
  waiting for transfers between devices  396 us (51%)
  blocking collectives  248 us (32%)
  matrix products  71 us (9%)
  local copies, waits for them, and re-layouts  30.1 us (4%)
  between operations  17 us (2%)
  other arithmetic  8.88 us (1%)
    reduce_scatter x1, waiting for transfers between devices, shards(): lax.psum_scatter(contribs.reshape(column_total, feature_count), 'blk', sc...  209 us
    all_gather x4, blocking collectives, merged(): everything = jax.tree.map(lambda part: lax.all_gather(part, axis), value)  167 us
    all_gather x1, waiting for transfers between devices, shards(): lax.all_gather(curve_emb, 'blk', axis=0, tiled=True)  107 us
    psum x1, blocking collectives, shards(): lax.psum(partial_value, ('blk', 'rep')) / (2.0 * column_total * rep_count)  80.9 us
    reduce_scatter x1, waiting for transfers between devices, shards(): lax.psum_scatter(running * logit_gain, 'rep', scatter_dimension=0, tiled=...  52.6 us
    dynamic_slice x34, local copies, waits for them, and re-layouts, lap(): return combine(so_far, jax.tree.map(lambda part: part[k], everything))  29 us
    dot_general x9, matrix products, scores_of(): jnp.einsum('rd,cd->rc', row_block, columns, preferred_element_type=jnp.fl...  27.3 us
    dot_general x8, matrix products, back_step(): jnp.einsum('rc,rd->cd', weight, image_block, preferred_element_type=jnp.f...  26.3 us
  transfers between devices with their start and end apart: 4, of which 4 were waited for; matrix products, arithmetic and copies ran while one was open for 0% of the time, Pallas kernels for 0%

commit v1 on v0

v1 whole, which is shorter than its diff:
```python
import functools
import math

import jax
import jax.numpy as jnp
from jax import lax
from jax.experimental import pallas as pl
from jax.experimental.pallas import tpu as pltpu
from jax.sharding import PartitionSpec as P

F32, BF16 = jnp.float32, jnp.bfloat16
MESH = pl.DeviceIdType.MESH
HOPS = (2, 1, 3)


def nt(a, b):
    return lax.dot_general(a, b, (((1,), (1,)), ((), ())), preferred_element_type=F32)


def nn(a, b):
    return lax.dot_general(a, b, (((1,), (0,)), ((), ())), preferred_element_type=F32)


def tn(a, b):
    return lax.dot_general(a, b, (((0,), (0,)), ((), ())), preferred_element_type=F32)


def kernel(
    gain,
    pairs,
    img_ref,
    cur_ref,
    loss_ref,
    dimg_ref,
    dcur_ref,
    I,
    C,
    S,
    W,
    rst,
    cst,
    tot_r,
    tot_c,
    val_r,
    val_c,
    pw,
    pin,
    pown,
    py,
    pyin,
    qo,
    qoin,
    qw,
    qin,
    qown,
    qy,
    qyin,
    ag_i_s,
    ag_i_r,
    ag_c_s,
    ag_c_r,
    co_s,
    co_r,
    st_r_s,
    st_r_r,
    st_c_s,
    st_c_r,
    vl_r_s,
    vl_r_r,
    vl_c_s,
    vl_c_r,
    px_s,
    px_r,
    py_s,
    py_r,
    qo_s,
    qo_r,
    qz_s,
    qz_r,
    qy_s,
    qy_r,
):
    blk, rep = lax.axis_index("blk"), lax.axis_index("rep")
    x = blk % 4
    z = (blk // 4) % 4
    yh = blk // 16
    yl = rep // 2
    c = rep % 2

    def dev(x, yl, z, yh, c):
        return ((yh * 4 + z) * 4 + x, yl * 2 + c)

    def img_dev(dx, dy):
        return dev((x + dx) % 4, (yl + dy) % 2, z, yh, c)

    def cur_dev(dz, dy, dc):
        return dev(x, yl, (z + dz) % 4, (yh + dy) % 2, (c + dc) % 2)

    def copy(src, dst, send, recv, device):
        return pltpu.make_async_remote_copy(
            src_ref=src, dst_ref=dst, send_sem=send, recv_sem=recv, device_id=device, device_id_type=MESH
        )

    img_peers = [(dx, dy) for dx in range(4) for dy in range(2) if dx or dy]
    cur_peers = [(dz, dy, dc) for dz in range(4) for dy in range(2) for dc in range(2) if dz or dy or dc]
    mi = x * 2 + yl
    mc = c * 8 + z * 2 + yh
    half = c * 8
    other = (1 - c) * 8

    barrier = pltpu.get_barrier_semaphore()
    for d in img_peers:
        pl.semaphore_signal(barrier, inc=1, device_id=img_dev(*d), device_id_type=MESH)
    for d in cur_peers:
        pl.semaphore_signal(barrier, inc=1, device_id=cur_dev(*d), device_id_type=MESH)
    pl.semaphore_wait(barrier, len(img_peers) + len(cur_peers))

    pending = []

    def go(cp):
        cp.start()
        pending.append(cp)
        return cp

    iy = go(copy(img_ref, I.at[mi], ag_i_s.at[0], ag_i_r.at[0], img_dev(0, 1)))
    cy = go(copy(cur_ref, C.at[mc], ag_c_s.at[0], ag_c_r.at[0], cur_dev(0, 1, 0)))
    ix, cz = {}, {}
    for d in (1, 3, 2):
        ix[d] = go(copy(img_ref, I.at[mi], ag_i_s.at[d], ag_i_r.at[d], img_dev(d, 0)))
        cz[d] = go(copy(cur_ref, C.at[mc], ag_c_s.at[d], ag_c_r.at[d], cur_dev(d, 0, 0)))
    cores = []

    def forward(slot, k):
        cores.append(go(copy(C.at[slot], C.at[slot], co_s.at[k], co_r.at[k], cur_dev(0, 0, 1))))

    cores.append(go(copy(cur_ref, C.at[mc], co_s.at[0], co_r.at[0], cur_dev(0, 0, 1))))
    I[mi] = img_ref[...]
    C[mc] = cur_ref[...]
    pos = jnp.sum(img_ref[...].astype(F32) * cur_ref[...].astype(F32), axis=1, keepdims=True) * gain
    pos = jnp.sum(pos, axis=0, keepdims=True)
    iy.wait_recv()
    si = x * 2 + 1 - yl
    sc = half + z * 2 + 1 - yh
    for d in (1, 3, 2):
        ix[d + 4] = go(copy(I.at[si], I.at[si], ag_i_s.at[d + 4], ag_i_r.at[d + 4], img_dev(d, 0)))
    cy.wait_recv()
    for d in (1, 3, 2):
        cz[d + 4] = go(copy(C.at[sc], C.at[sc], ag_c_s.at[d + 4], ag_c_r.at[d + 4], cur_dev(d, 0, 0)))
    forward(sc, 1)
    k = 2
    for y, off in ((yh, 0), (1 - yh, 4)):
        for d in (1, 3, 2):
            cz[d + off].wait_recv()
            forward(half + ((z - d) % 4) * 2 + y, k)
            k += 1
    for d in (1, 3, 2, 5, 7, 6):
        ix[d].wait_recv()
    for cp in cores:
        cp.wait_recv()

    def score_step(p, carry):
        cols = C[pl.ds(2 * p, 2)].reshape(256, 1024)
        s = nt(I[...].reshape(1024, 1024), cols) * gain
        S[p] = s
        high = jnp.max(s, axis=0, keepdims=True)
        lse = high + jnp.log(jnp.sum(jnp.exp(s - high), axis=0, keepdims=True))
        cst[mc, pl.ds(2 * p, 1), :] = lse[:, :128]
        cst[mc, pl.ds(2 * p + 1, 1), :] = lse[:, 128:]
        return carry

    lax.fori_loop(0, 8, score_step, 0)
    c_st = []
    for j, d in enumerate(cur_peers):
        c_st.append(go(copy(cst.at[mc], cst.at[mc], st_c_s.at[j], st_c_r.at[j], cur_dev(*d))))

    def chunks(a):
        rows = pl.ds(pl.multiple_of(a * 128, 128), 128)
        return [S[p, rows, h * 128 : (h + 1) * 128] for p in range(8) for h in range(2)]

    def row_step(a, carry):
        parts = chunks(a)
        m = functools.reduce(jnp.maximum, parts)
        total = functools.reduce(jnp.add, [jnp.exp(v - m) for v in parts])
        mt, lt = m.T, total.T
        high = jnp.max(mt, axis=0, keepdims=True)
        lse = high + jnp.log(jnp.sum(lt * jnp.exp(mt - high), axis=0, keepdims=True))
        rst[mi, pl.ds(a, 1), :] = lse
        return carry

    lax.fori_loop(0, 8, row_step, 0)
    rst[mi, 8:16, :] = jnp.broadcast_to(pos, (8, 128))
    r_st = []
    for j, d in enumerate(img_peers):
        r_st.append(go(copy(rst.at[mi], rst.at[mi], st_r_s.at[j], st_r_r.at[j], img_dev(*d))))
    for cp in c_st:
        cp.wait_recv()
    parts = [cst[k] for k in range(16)]
    high = functools.reduce(jnp.maximum, parts)
    tot_c[...] = high + jnp.log(functools.reduce(jnp.add, [jnp.exp(v - high) for v in parts]))
    for cp in r_st:
        cp.wait_recv()
    parts = [rst[k, 0:8, :] for k in range(8)]
    high = functools.reduce(jnp.maximum, parts)
    tot_r[...] = high + jnp.log(functools.reduce(jnp.add, [jnp.exp(v - high) for v in parts]))

    def grand(v):
        return jnp.sum(jnp.sum(v, axis=1, keepdims=True), axis=0, keepdims=True)

    pos_all = functools.reduce(jnp.add, [rst[k, 8:16, :] for k in range(8)])
    val_c[mc] = grand(tot_r[...]) - 2.0 * pos_all
    val_r[mi] = jnp.broadcast_to(grand(tot_c[...]), (8, 128))
    vals = []
    for j, d in enumerate(cur_peers):
        vals.append(go(copy(val_c.at[mc], val_c.at[mc], vl_c_s.at[j], vl_c_r.at[j], cur_dev(*d))))
    for j, d in enumerate(img_peers):
        vals.append(go(copy(val_r.at[mi], val_r.at[mi], vl_r_s.at[j], vl_r_r.at[j], img_dev(*d))))

    def weight_step(a, carry):
        rows = pl.ds(pl.multiple_of(a * 128, 128), 128)
        rl = jnp.broadcast_to(tot_r[pl.ds(a, 1), :], (128, 128)).T
        for p in range(8):
            for h in range(2):
                lanes = slice(h * 128, (h + 1) * 128)
                s = S[p, rows, lanes]
                cl = tot_c[2 * p + h : 2 * p + h + 1, :]
                W[p, rows, lanes] = ((jnp.exp(s - rl) + jnp.exp(s - cl)) * 0.5).astype(BF16)
        return carry

    lax.fori_loop(0, 8, weight_step, 0)

    def curve_part(pair):
        return tn(W[pair], I[...].reshape(1024, 1024))

    qos = []
    for j, d in enumerate((2, 1, 3, 0)):
        zz = (z + d) % 4
        qo[j] = curve_part((1 - c) * 4 + zz).reshape(2, 128, 1024)
        qos.append(go(copy(qo.at[j], qoin.at[j], qo_s.at[j], qo_r.at[j], cur_dev(0, 0, 1))))

    def image_part(xx):
        rows = pl.ds(pl.multiple_of(xx * 256, 256), 256)
        w = jnp.concatenate([W[p, rows, :] for p in range(8)], axis=1)
        return nn(w, C[...].reshape(2048, 1024))

    pxs = []
    for j, d in enumerate(HOPS):
        pw[j] = image_part((x + d) % 4).astype(BF16).reshape(2, 128, 1024)
        pxs.append(go(copy(pw.at[j], pin.at[j], px_s.at[j], px_r.at[j], img_dev(d, 0))))
    pown[...] = image_part(x).reshape(2, 128, 1024)
    qzs = []
    for j, d in enumerate(HOPS):
        part = curve_part(c * 4 + (z + d) % 4).reshape(2, 128, 1024)
        qos[j].wait_recv()
        qw[j] = (part + qoin[j]).astype(BF16)
        qzs.append(go(copy(qw.at[j], qin.at[j], qz_s.at[j], qz_r.at[j], cur_dev(d, 0, 0))))
    part = curve_part(c * 4 + z).reshape(2, 128, 1024)
    qos[3].wait_recv()
    qown[...] = part + qoin[3]

    for cp in pxs:
        cp.wait_recv()
    py[...] = (pown[1 - yl] + sum(pin[j, 1 - yl].astype(F32) for j in range(3))).astype(BF16)
    pys = go(copy(py, pyin, py_s, py_r, img_dev(0, 1)))
    for cp in qzs:
        cp.wait_recv()
    qy[...] = (qown[1 - yh] + sum(qin[j, 1 - yh].astype(F32) for j in range(3))).astype(BF16)
    qys = go(copy(qy, qyin, qy_s, qy_r, cur_dev(0, 1, 0)))
    mine = pown[yl] + sum(pin[j, yl].astype(F32) for j in range(3)) - cur_ref[...].astype(F32)
    pys.wait_recv()
    dimg_ref[...] = (mine + pyin[...].astype(F32)) * gain
    mine = qown[yh] + sum(qin[j, yh].astype(F32) for j in range(3)) - img_ref[...].astype(F32)
    for cp in vals:
        cp.wait_recv()
    total = sum(val_c[k] for k in range(16)) + sum(val_r[k] for k in range(8))
    loss_ref[...] = total[0:1, 0:1] / (2.0 * pairs)
    qys.wait_recv()
    dcur_ref[...] = (mine + qyin[...].astype(F32)) * gain
    for cp in pending:
        cp.wait_send()


def solution(mesh):
    def step(image_emb, curve_emb):
        gain = math.sqrt(image_emb.shape[1])
        vmem = pl.BlockSpec(memory_space=pltpu.VMEM)
        dma = pltpu.SemaphoreType.DMA
        loss, dimg, dcur = pl.pallas_call(
            functools.partial(kernel, gain, 16384),
            out_shape=(
                jax.ShapeDtypeStruct((1, 1), F32),
                jax.ShapeDtypeStruct((128, 1024), F32),
                jax.ShapeDtypeStruct((128, 1024), F32),
            ),
            in_specs=[vmem, vmem],
            out_specs=(vmem, vmem, vmem),
            scratch_shapes=[
                pltpu.VMEM((8, 128, 1024), BF16),
                pltpu.VMEM((16, 128, 1024), BF16),
                pltpu.VMEM((8, 1024, 256), F32),
                pltpu.VMEM((8, 1024, 256), BF16),
                pltpu.VMEM((8, 16, 128), F32),
                pltpu.VMEM((16, 16, 128), F32),
                pltpu.VMEM((8, 128), F32),
                pltpu.VMEM((16, 128), F32),
                pltpu.VMEM((8, 8, 128), F32),
                pltpu.VMEM((16, 8, 128), F32),
                pltpu.VMEM((3, 2, 128, 1024), BF16),
                pltpu.VMEM((3, 2, 128, 1024), BF16),
                pltpu.VMEM((2, 128, 1024), F32),
                pltpu.VMEM((128, 1024), BF16),
                pltpu.VMEM((128, 1024), BF16),
                pltpu.VMEM((4, 2, 128, 1024), F32),
                pltpu.VMEM((4, 2, 128, 1024), F32),
                pltpu.VMEM((3, 2, 128, 1024), BF16),
                pltpu.VMEM((3, 2, 128, 1024), BF16),
                pltpu.VMEM((2, 128, 1024), F32),
                pltpu.VMEM((128, 1024), BF16),
                pltpu.VMEM((128, 1024), BF16),
                dma((8,)), dma((8,)), dma((8,)), dma((8,)), dma((8,)), dma((8,)),
                dma((7,)), dma((7,)), dma((15,)), dma((15,)),
                dma((7,)), dma((7,)), dma((15,)), dma((15,)),
                dma((3,)), dma((3,)), dma, dma,
                dma((4,)), dma((4,)), dma((3,)), dma((3,)), dma, dma,
            ],
            compiler_params=pltpu.CompilerParams(
                collective_id=0, has_side_effects=True, vmem_limit_bytes=60 << 20
            ),
        )(image_emb, curve_emb)
        return loss.reshape(()), dimg, dcur

    spec = P(("blk", "rep"), None)
    return jax.shard_map(step, mesh=mesh, in_specs=(spec, spec), out_specs=(P(), spec, spec), check_vma=False)
```

time: 774 us -> 106 us (0.14)
  waiting for transfers between devices: 396 us -> 0 us
  blocking collectives: 248 us -> 0 us
  Pallas kernels: 0 us -> 101 us
  matrix products: 71 us -> 0 us
  local copies, waits for them, and re-layouts: 30.1 us -> 2.74 us
  between operations: 17 us -> 2.41 us
  other arithmetic: 8.88 us -> 0 us
    reduce_scatter x2 -> x0, waiting for transfers between devices: 262 us -> none  [the longest x1 209 us: shards(): lax.psum_scatter(contribs.reshape(column_total, feature_count), 'blk', sc...]
    all_gather x4 -> x0, blocking collectives: 167 us -> none  [merged(): everything = jax.tree.map(lambda part: lax.all_gather(part, axis), value)]
    all_gather x2 -> x0, waiting for transfers between devices: 133 us -> none  [the longest x1 107 us: shards(): lax.all_gather(curve_emb, 'blk', axis=0, tiled=True)]
    pallas_call x0 -> x1, Pallas kernels: none -> 101 us  [step(): pl.pallas_call(functools.partial(kernel, gain, 16384), out_shape=(jax.Sha...]
    psum x1 -> x0, blocking collectives: 80.9 us -> none  [shards(): lax.psum(partial_value, ('blk', 'rep')) / (2.0 * column_total * rep_count)]
    dot_general x25 -> x0, matrix products: 71 us -> none  [the longest x9 27.3 us: scores_of(): jnp.einsum('rd,cd->rc', row_block, columns, preferred_element_type=jnp.fl...]
    dynamic_slice x42 -> x0, local copies, waits for them, and re-layouts: 29.1 us -> none  [the longest x34 29 us: lap(): return combine(so_far, jax.tree.map(lambda part: part[k], everything))]
  transfers between devices with their start and end apart: 4 -> 0, of which waited for: 4 -> 0; matrix products, arithmetic and copies ran while one was open for 0% -> 0% of each run, Pallas kernels for 0% -> 0%
where the time goes in v1:
time: 106 us
  Pallas kernels  101 us (95%)
  local copies, waits for them, and re-layouts  2.74 us (3%)
  between operations  2.41 us (2%)
    pallas_call x1, Pallas kernels, step(): pl.pallas_call(functools.partial(kernel, gain, 16384), out_shape=(jax.Sha...  101 us
    unnamed x4, local copies, waits for them, and re-layouts  2.74 us

profile of v1, /device:TPU:1, one launch (start us, length us, event | category | flops | bytes accessed | tf_op | source)
XLA Modules:
  0.0 105.7 jit_solution(2909608509730373989)
XLA Ops:
  0.6 100.5 %shard_map.49 = (f32[1,1]{1,0:T(1,128)}, f32[128,1024]{1,0:T(8,128)}, f32[128,1024]{1,0:T(8,128)}) custom-call(bf16[128,1024]{1,0:T(8,128)(2,1)} %img_ref.1, bf16[128,1024]{1,0:T(8,128)(2,1)} %cur_ref.1), custom_call_target="tpu_custom_call" | custom-call | tf_op jit(solution)/shard_map/pallas_call | solution.py:287
  101.8 0.0 copy-start
  101.8 1.9 %copy.9 = f32[128,1024]{1,0:T(8,128)} copy(f32[128,1024]{1,0:T(8,128)} %get-tuple-element.13) | data formatting | bytes 1048576
  103.8 0.0 copy-done
  103.8 0.8 copy.10
Async XLA Ops:
  101.8 2.0 %copy-start = (f32[128,1024]{1,0:T(8,128)S(1)}, f32[128,1024]{1,0:T(8,128)}, u32[]{:S(2)}) copy-start(f32[128,1024]{1,0:T(8,128)} %get-tuple-element.14) | copy-start | bytes 1572868

commit v2 on v1

v2 whole, which is shorter than its diff:
```python
import functools
import math

import jax
import jax.numpy as jnp
from jax import lax
from jax.experimental import pallas as pl
from jax.experimental.pallas import tpu as pltpu
from jax.sharding import PartitionSpec as P

F32, BF16 = jnp.float32, jnp.bfloat16
MESH = pl.DeviceIdType.MESH
PLACES = ((0, 0), (0, 1), (-1, 0), (1, 0), (2, 0), (-1, 1), (1, 1), (2, 1))
SLOT = {p: k for k, p in enumerate(PLACES)}
HALF = (slice(0, 64), slice(64, 128))
COPIES = 128


def nt(a, b):
    return lax.dot_general(a, b, (((1,), (1,)), ((), ())), preferred_element_type=F32)


def nn(a, b):
    return lax.dot_general(a, b, (((1,), (0,)), ((), ())), preferred_element_type=F32)


def tn(a, b):
    return lax.dot_general(a, b, (((0,), (0,)), ((), ())), preferred_element_type=F32)


def kernel(
    gain,
    pairs,
    img_ref,
    cur_ref,
    loss_ref,
    dimg_ref,
    dcur_ref,
    I,
    C,
    S,
    W,
    RM,
    RL,
    CM,
    CL,
    rst,
    cst,
    tot_r,
    tot_c,
    val_r,
    val_c,
    pw,
    pin,
    pf,
    pown,
    py,
    qo,
    qoin,
    qw,
    qin,
    qf,
    qown,
    qy,
    sends,
    recvs,
):
    blk, rep = lax.axis_index("blk"), lax.axis_index("rep")
    x = blk % 4
    z = (blk // 4) % 4
    yh = blk // 16
    yl = rep // 2
    c = rep % 2

    def dev(x, yl, z, yh, c):
        return ((yh * 4 + z) * 4 + x, yl * 2 + c)

    def img_dev(dx, dy):
        return dev((x + dx + 4) % 4, (yl + dy) % 2, z, yh, c)

    def cur_dev(dz, dy, dc):
        return dev(x, (yl + dy) % 2, (z + dz + 4) % 4, (yh + dy) % 2, (c + dc) % 2)

    count = [0]
    pending = []

    def go(src, dst, device):
        k = count[0]
        count[0] += 1
        cp = pltpu.make_async_remote_copy(
            src_ref=src,
            dst_ref=dst,
            send_sem=sends.at[k],
            recv_sem=recvs.at[k],
            device_id=device,
            device_id_type=MESH,
        )
        cp.start()
        pending.append(cp)
        return cp

    img_peers = [(dx, dy) for dx in range(4) for dy in range(2) if dx or dy]
    cur_peers = [(dz, dy, dc) for dz in range(4) for dy in range(2) for dc in range(2) if dz or dy or dc]

    barrier = pltpu.get_barrier_semaphore()
    near = [img_dev(0, 1), img_dev(1, 0), img_dev(-1, 0)]
    near += [cur_dev(0, 1, 0), cur_dev(1, 0, 0), cur_dev(-1, 0, 0), cur_dev(0, 0, 1)]
    for d in near:
        pl.semaphore_signal(barrier, inc=1, device_id=d, device_id_type=MESH)
    pl.semaphore_wait(barrier, len(near))

    ring = ((1, 0), (-1, 1))
    back = ((1, 1), (-1, 0))
    iy, cy, io, co, ip, cp_, ir, cr = ({} for _ in range(8))
    cores = {}

    def core(slot, h):
        cores[slot, h] = go(C.at[slot, 0, HALF[h]], C.at[slot, 1, HALF[h]], cur_dev(0, 0, 1))

    def send_own(d, h):
        s = SLOT[-d, 0]
        io[d, h] = go(img_ref.at[HALF[h]], I.at[s, HALF[h]], img_dev(d, 0))
        co[d, h] = go(cur_ref.at[HALF[h]], C.at[s, 0, HALF[h]], cur_dev(d, 0, 0))

    def pass_on(d, h, y):
        s, t = SLOT[-d, y], SLOT[2, y]
        ir[d, h, y] = go(I.at[s, HALF[h]], I.at[t, HALF[h]], img_dev(d, 0))
        cr[d, h, y] = go(C.at[s, 0, HALF[h]], C.at[t, 0, HALF[h]], cur_dev(d, 0, 0))

    for h in range(2):
        iy[h] = go(img_ref.at[HALF[h]], I.at[1, HALF[h]], img_dev(0, 1))
        cy[h] = go(cur_ref.at[HALF[h]], C.at[1, 0, HALF[h]], cur_dev(0, 1, 0))
        for d, k in ring if h == 0 else back:
            send_own(d, k)
    own_core = go(cur_ref, C.at[0, 1], cur_dev(0, 0, 1))
    I[0] = img_ref[...]
    C[0, 0] = cur_ref[...]
    pos = jnp.sum(img_ref[...].astype(F32) * cur_ref[...].astype(F32), axis=1, keepdims=True) * gain
    pos = jnp.sum(pos, axis=0, keepdims=True)
    for d, h in ring:
        io[d, h].wait_recv()
        co[d, h].wait_recv()
        pass_on(d, h, 0)
        core(SLOT[-d, 0], h)
    for h in range(2):
        iy[h].wait_recv()
        cy[h].wait_recv()
        for d, k in ring if h == 0 else back:
            ip[d, h] = go(I.at[1, HALF[h]], I.at[SLOT[-d, 1], HALF[h]], img_dev(d, 0))
            cp_[d, h] = go(C.at[1, 0, HALF[h]], C.at[SLOT[-d, 1], 0, HALF[h]], cur_dev(d, 0, 0))
        core(1, h)
        if h == 0:
            for d, k in back:
                io[d, k].wait_recv()
                co[d, k].wait_recv()
                core(SLOT[-d, 0], k)

    def scores(rows, cols):
        r0, r1 = rows

        def step(q, carry):
            a = I[r0:r1].reshape((r1 - r0) * 128, 1024)
            s = nt(a, C[q].reshape(256, 1024)) * gain
            S[q, r0:r1] = s.reshape(r1 - r0, 128, 256)
            return carry

        lax.fori_loop(cols[0], cols[1], step, 0)

    def row_stats(rows, cols, fresh):
        def step(a, carry):
            parts = [S[q, a, :, h * 128 : h * 128 + 128] for q in range(*cols) for h in range(2)]
            m = functools.reduce(jnp.maximum, parts)
            if fresh:
                total = functools.reduce(jnp.add, [jnp.exp(v - m) for v in parts])
            else:
                old = RM[a]
                m = jnp.maximum(m, old)
                total = RL[a] * jnp.exp(old - m)
                total = functools.reduce(jnp.add, [jnp.exp(v - m) for v in parts], total)
            RM[a] = m
            RL[a] = total
            return carry

        lax.fori_loop(rows[0], rows[1], step, 0)

    def col_stats(rows, cols, fresh):
        r0, r1 = rows

        def step(q, carry):
            s = S[q, r0:r1].reshape((r1 - r0) * 16, 8, 256)
            m = jnp.max(s, axis=0)
            if not fresh:
                old = CM[q]
                m = jnp.maximum(m, old)
            total = jnp.sum(jnp.exp(s - m[None]), axis=0)
            if not fresh:
                total = total + CL[q] * jnp.exp(old - m)
            CM[q] = m
            CL[q] = total
            return carry

        lax.fori_loop(cols[0], cols[1], step, 0)

    for d, h in ring + back:
        cores[SLOT[-d, 0], h].wait_recv()
    own_core.wait_recv()
    cores[1, 0].wait_recv()
    cores[1, 1].wait_recv()
    scores((0, 4), (0, 4))
    row_stats((0, 4), (0, 4), True)
    col_stats((0, 4), (0, 4), True)
    for d, h in ring:
        ir[d, h, 0].wait_recv()
        cr[d, h, 0].wait_recv()
        core(SLOT[2, 0], h)
    for d, h in ring:
        ip[d, h].wait_recv()
        cp_[d, h].wait_recv()
        pass_on(d, h, 1)
        core(SLOT[-d, 1], h)
    for d, h in back:
        ip[d, h].wait_recv()
        cp_[d, h].wait_recv()
        core(SLOT[-d, 1], h)
    for d, h in ring + back:
        cores[SLOT[-d, 1], h].wait_recv()
    for h in range(2):
        cores[SLOT[2, 0], h].wait_recv()
    scores((4, 7), (0, 4))
    scores((0, 7), (4, 7))
    for d, h in ring:
        ir[d, h, 1].wait_recv()
        cr[d, h, 1].wait_recv()
        core(SLOT[2, 1], h)
    row_stats((0, 4), (4, 7), False)
    row_stats((4, 7), (0, 7), True)
    col_stats((4, 7), (0, 4), False)
    col_stats((0, 7), (4, 7), True)
    for h in range(2):
        cores[SLOT[2, 1], h].wait_recv()
    scores((7, 8), (0, 7))
    scores((0, 8), (7, 8))
    row_stats((0, 7), (7, 8), False)
    row_stats((7, 8), (0, 8), True)
    col_stats((7, 8), (0, 7), False)
    col_stats((0, 8), (7, 8), True)

    def img_place(dx, dy):
        return ((x + dx + 4) % 4) * 2 + (yl + dy) % 2

    def cur_place(dz, dy, dc):
        return ((c + dc) % 2) * 8 + ((z + dz + 4) % 4) * 2 + (yh + dy) % 2

    mi = img_place(0, 0)
    mc = cur_place(0, 0, 0)
    for q, (dz, dy) in enumerate(PLACES):
        m = CM[q]
        high = jnp.max(m, axis=0, keepdims=True)
        lse = high + jnp.log(jnp.sum(CL[q] * jnp.exp(m - high), axis=0, keepdims=True))
        cst[mc, pl.ds(cur_place(dz, dy, 0), 1), :] = lse[:, :128]
        cst[mc, pl.ds(cur_place(dz, dy, 1), 1), :] = lse[:, 128:]
    c_st = [go(cst.at[mc], cst.at[mc], cur_dev(*d)) for d in cur_peers]
    for a, (dx, dy) in enumerate(PLACES):
        m = RM[a].T
        high = jnp.max(m, axis=0, keepdims=True)
        lse = high + jnp.log(jnp.sum(RL[a].T * jnp.exp(m - high), axis=0, keepdims=True))
        rst[mi, pl.ds(img_place(dx, dy), 1), :] = lse
    rst[mi, 8:16, :] = jnp.broadcast_to(pos, (8, 128))
    r_st = [go(rst.at[mi], rst.at[mi], img_dev(*d)) for d in img_peers]
    for cp in r_st:
        cp.wait_recv()
    parts = [rst[k, 0:8, :] for k in range(8)]
    high = functools.reduce(jnp.maximum, parts)
    tot_r[...] = high + jnp.log(functools.reduce(jnp.add, [jnp.exp(v - high) for v in parts]))
    for a, (dx, dy) in enumerate(PLACES):
        RM[a] = jnp.broadcast_to(tot_r[pl.ds(img_place(dx, dy), 1), :], (128, 128)).T
    for cp in c_st:
        cp.wait_recv()
    parts = [cst[k] for k in range(16)]
    high = functools.reduce(jnp.maximum, parts)
    tot_c[...] = high + jnp.log(functools.reduce(jnp.add, [jnp.exp(v - high) for v in parts]))

    for q, (dz, dy) in enumerate(PLACES):
        for h in range(2):
            CM[q, :, h * 128 : h * 128 + 128] = jnp.broadcast_to(tot_c[pl.ds(cur_place(dz, dy, h), 1), :], (8, 128))

    def weight_step(a, carry):
        rl = RM[a]
        for q in range(8):
            for h in range(2):
                lanes = slice(h * 128, h * 128 + 128)
                s = S[q, a, :, lanes]
                cl = CM[q, 0:1, lanes]
                W[q, a, :, lanes] = ((jnp.exp(s - rl) + jnp.exp(s - cl)) * 0.5).astype(BF16)
        return carry

    lax.fori_loop(0, 8, weight_step, 0)

    swaps = {}
    curve_f32 = {}

    def curve_part(q):
        part = tn(W[q].reshape(1024, 256), I[...].reshape(1024, 1024))
        qo[q, 1] = part[128:256]
        swaps[q] = go(qo.at[q, 1], qoin.at[q], cur_dev(0, 0, 1))
        qo[q, 0] = part[0:128]

    def joined(q):
        swaps[q].wait_recv()
        return qo[q, 0] + qoin[q]

    def image_part(a1, a2):
        w = jnp.concatenate(
            [jnp.concatenate([W[q, a] for q in range(8)], axis=1) for a in (a1, a2)], axis=0
        )
        return nn(w, C[...].reshape(2048, 1024))

    hops = {}

    def far(kind, y, part):
        w, into, to = (pw, pin, lambda d: img_dev(d, 0)) if kind == "i" else (qw, qin, lambda d: cur_dev(d, 0, 0))
        w[y, 0] = part.astype(BF16)
        for d, h in ring:
            hops[kind, y, "far", d] = go(w.at[y, 0, HALF[h]], into.at[y, 0, HALF[h]], to(d))

    def near_first(kind, y, d, part):
        w, into, keep, to = (
            (pw, pin, pf, lambda d: img_dev(d, 0)) if kind == "i" else (qw, qin, qf, lambda d: cur_dev(d, 0, 0))
        )
        k = 1 if d == 1 else 2
        through = 0 if d == 1 else 1
        rest = 1 - through
        w[y, k, HALF[rest]] = part[HALF[rest]].astype(BF16)
        hops[kind, y, "rest", d] = go(w.at[y, k, HALF[rest]], into.at[y, k, HALF[rest]], to(d))
        keep[y, k - 1] = part[HALF[through]]

    def near_second(kind, y):
        w, into, keep, to = (
            (pw, pin, pf, lambda d: img_dev(d, 0)) if kind == "i" else (qw, qin, qf, lambda d: cur_dev(d, 0, 0))
        )
        for d, h in ring:
            k = 1 if d == 1 else 2
            hops[kind, y, "far", d].wait_recv()
            w[y, k, HALF[h]] = (keep[y, k - 1] + into[y, 0, HALF[h]].astype(F32)).astype(BF16)
            hops[kind, y, "through", d] = go(w.at[y, k, HALF[h]], into.at[y, k, HALF[h]], to(d))

    def collected(kind, y):
        into, own = (pin, pown) if kind == "i" else (qin, qown)
        for d in (1, -1):
            hops[kind, y, "rest", d].wait_recv()
            hops[kind, y, "through", d].wait_recv()
        return own[y] + into[y, 1].astype(F32) + into[y, 2].astype(F32)

    curve_part(SLOT[2, 1])
    curve_part(SLOT[2, 0])
    part = image_part(SLOT[2, 1], SLOT[2, 0])
    far("i", 1, part[0:128])
    far("i", 0, part[128:256])
    curve_part(SLOT[1, 1])
    curve_part(SLOT[-1, 1])
    far("c", 1, joined(SLOT[2, 1]))
    far("c", 0, joined(SLOT[2, 0]))
    part = image_part(SLOT[1, 1], SLOT[-1, 1])
    near_first("i", 1, 1, part[0:128])
    near_first("i", 1, -1, part[128:256])
    near_first("c", 1, 1, joined(SLOT[1, 1]))
    near_first("c", 1, -1, joined(SLOT[-1, 1]))
    curve_part(SLOT[1, 0])
    curve_part(SLOT[-1, 0])
    near_second("i", 1)
    part = image_part(SLOT[1, 0], SLOT[-1, 0])
    near_first("i", 0, 1, part[0:128])
    near_first("i", 0, -1, part[128:256])
    near_second("c", 1)
    near_first("c", 0, 1, joined(SLOT[1, 0]))
    near_first("c", 0, -1, joined(SLOT[-1, 0]))
    curve_part(SLOT[0, 1])
    curve_part(SLOT[0, 0])
    near_second("i", 0)
    near_second("c", 0)
    part = image_part(SLOT[0, 1], SLOT[0, 0])
    pown[1] = part[0:128]
    pown[0] = part[128:256]
    qown[1] = joined(SLOT[0, 1])
    qown[0] = joined(SLOT[0, 0])

    py[0] = collected("i", 1).astype(BF16)
    pys = go(py.at[0], py.at[1], img_dev(0, 1))
    qy[0] = collected("c", 1).astype(BF16)
    qys = go(qy.at[0], qy.at[1], cur_dev(0, 1, 0))

    def grand(v):
        return jnp.sum(jnp.sum(v, axis=1, keepdims=True), axis=0, keepdims=True)

    pos_all = functools.reduce(jnp.add, [rst[k, 8:16, :] for k in range(8)])
    val_c[mc] = grand(tot_r[...]) - 2.0 * pos_all
    val_r[mi] = jnp.broadcast_to(grand(tot_c[...]), (8, 128))
    vals = [go(val_c.at[mc], val_c.at[mc], cur_dev(*d)) for d in cur_peers]
    vals += [go(val_r.at[mi], val_r.at[mi], img_dev(*d)) for d in img_peers]

    pown[0] = collected("i", 0) - cur_ref[...].astype(F32)
    qown[0] = collected("c", 0) - img_ref[...].astype(F32)
    for cp in vals:
        cp.wait_recv()
    total = sum(val_c[k] for k in range(16)) + sum(val_r[k] for k in range(8))
    loss_ref[...] = total[0:1, 0:1] / (2.0 * pairs)
    pys.wait_recv()
    dimg_ref[...] = (pown[0] + py[1].astype(F32)) * gain
    qys.wait_recv()
    dcur_ref[...] = (qown[0] + qy[1].astype(F32)) * gain
    for cp in pending:
        cp.wait_send()


def solution(mesh):
    def step(image_emb, curve_emb):
        gain = math.sqrt(image_emb.shape[1])
        vmem = pl.BlockSpec(memory_space=pltpu.VMEM)
        loss, dimg, dcur = pl.pallas_call(
            functools.partial(kernel, gain, 16384),
            out_shape=(
                jax.ShapeDtypeStruct((1, 1), F32),
                jax.ShapeDtypeStruct((128, 1024), F32),
                jax.ShapeDtypeStruct((128, 1024), F32),
            ),
            in_specs=[vmem, vmem],
            out_specs=(vmem, vmem, vmem),
            scratch_shapes=[
                pltpu.VMEM((8, 128, 1024), BF16),
                pltpu.VMEM((8, 2, 128, 1024), BF16),
                pltpu.VMEM((8, 8, 128, 256), F32),
                pltpu.VMEM((8, 8, 128, 256), BF16),
                pltpu.VMEM((8, 128, 128), F32),
                pltpu.VMEM((8, 128, 128), F32),
                pltpu.VMEM((8, 8, 256), F32),
                pltpu.VMEM((8, 8, 256), F32),
                pltpu.VMEM((8, 16, 128), F32),
                pltpu.VMEM((16, 16, 128), F32),
                pltpu.VMEM((8, 128), F32),
                pltpu.VMEM((16, 128), F32),
                pltpu.VMEM((8, 8, 128), F32),
                pltpu.VMEM((16, 8, 128), F32),
                pltpu.VMEM((2, 3, 128, 1024), BF16),
                pltpu.VMEM((2, 3, 128, 1024), BF16),
                pltpu.VMEM((2, 2, 64, 1024), F32),
                pltpu.VMEM((2, 128, 1024), F32),
                pltpu.VMEM((2, 128, 1024), BF16),
                pltpu.VMEM((8, 2, 128, 1024), F32),
                pltpu.VMEM((8, 128, 1024), F32),
                pltpu.VMEM((2, 3, 128, 1024), BF16),
                pltpu.VMEM((2, 3, 128, 1024), BF16),
                pltpu.VMEM((2, 2, 64, 1024), F32),
                pltpu.VMEM((2, 128, 1024), F32),
                pltpu.VMEM((2, 128, 1024), BF16),
                pltpu.SemaphoreType.DMA((COPIES,)),
                pltpu.SemaphoreType.DMA((COPIES,)),
            ],
            compiler_params=pltpu.CompilerParams(
                collective_id=0, has_side_effects=True, vmem_limit_bytes=60 << 20
            ),
        )(image_emb, curve_emb)
        return loss.reshape(()), dimg, dcur

    spec = P(("blk", "rep"), None)
    return jax.shard_map(step, mesh=mesh, in_specs=(spec, spec), out_specs=(P(), spec, spec), check_vma=False)
```

time: 106 us -> 80.6 us (0.76)
  Pallas kernels: 101 us -> 75.3 us
    pallas_call x1, Pallas kernels: 101 us -> 75.3 us  [step(): pl.pallas_call(functools.partial(kernel, gain, 16384), out_shape=(jax.Sha...]
where the time goes in v2:
time: 80.6 us; the launch traced here: 80.5 us
  Pallas kernels  75.3 us (93%)
  local copies, waits for them, and re-layouts  2.74 us (3%)
  between operations  2.41 us (3%)
    pallas_call x1, Pallas kernels, step(): pl.pallas_call(functools.partial(kernel, gain, 16384), out_shape=(jax.Sha...  75.3 us
    unnamed x4, local copies, waits for them, and re-layouts  2.74 us

profile of v2, /device:TPU:1, one launch (start us, length us, event | category | flops | bytes accessed | tf_op | source)
XLA Modules:
  0.0 80.5 jit_solution(2224827947550946475)
XLA Ops:
  0.6 75.3 %shard_map.49 = (f32[1,1]{1,0:T(1,128)}, f32[128,1024]{1,0:T(8,128)}, f32[128,1024]{1,0:T(8,128)}) custom-call(bf16[128,1024]{1,0:T(8,128)(2,1)} %img_ref.1, bf16[128,1024]{1,0:T(8,128)(2,1)} %cur_ref.1), custom_call_target="tpu_custom_call" | custom-call | tf_op jit(solution)/shard_map/pallas_call | solution.py:419
  76.6 0.0 copy-start
  76.6 1.9 %copy.9 = f32[128,1024]{1,0:T(8,128)} copy(f32[128,1024]{1,0:T(8,128)} %get-tuple-element.13) | data formatting | bytes 1048576
  78.5 0.0 copy-done
  78.5 0.8 copy.10
Async XLA Ops:
  76.6 2.0 %copy-start = (f32[128,1024]{1,0:T(8,128)S(1)}, f32[128,1024]{1,0:T(8,128)}, u32[]{:S(2)}) copy-start(f32[128,1024]{1,0:T(8,128)} %get-tuple-element.14) | copy-start | bytes 1572868

commit v3 on v2

v3 whole, which is shorter than its diff:
```python
import functools
import math

import jax
import jax.numpy as jnp
from jax import lax
from jax.experimental import pallas as pl
from jax.experimental.pallas import tpu as pltpu
from jax.sharding import PartitionSpec as P

F32, BF16 = jnp.float32, jnp.bfloat16
MESH = pl.DeviceIdType.MESH
PLACES = ((0, 0), (0, 1), (-1, 0), (1, 0), (2, 0), (-1, 1), (1, 1), (2, 1))
SLOT = {p: k for k, p in enumerate(PLACES)}
HALF = (slice(0, 64), slice(64, 128))


def nt(a, b):
    return lax.dot_general(a, b, (((1,), (1,)), ((), ())), preferred_element_type=F32)


def nn(a, b):
    return lax.dot_general(a, b, (((1,), (0,)), ((), ())), preferred_element_type=F32)


def tn(a, b):
    return lax.dot_general(a, b, (((0,), (0,)), ((), ())), preferred_element_type=F32)


def kernel(
    gain,
    pairs,
    img_ref,
    cur_ref,
    loss_ref,
    dimg_ref,
    dcur_ref,
    I,
    C,
    S,
    W,
    RM,
    RL,
    CM,
    CL,
    rst,
    cst,
    tot_r,
    tot_c,
    val_r,
    val_c,
    pw,
    pin,
    pf,
    pa,
    pown,
    py,
    qo,
    qoin,
    qw,
    qin,
    qf,
    qa,
    qown,
    qy,
    sends,
    recvs,
):
    blk, rep = lax.axis_index("blk"), lax.axis_index("rep")
    x = blk % 4
    z = (blk // 4) % 4
    yh = blk // 16
    yl = rep // 2
    c = rep % 2

    def dev(x, yl, z, yh, c):
        return ((yh * 4 + z) * 4 + x, yl * 2 + c)

    def img_dev(dx, dy):
        return dev((x + dx + 4) % 4, (yl + dy) % 2, z, yh, c)

    def cur_dev(dz, dy, dc):
        return dev(x, (yl + dy) % 2, (z + dz + 4) % 4, (yh + dy) % 2, (c + dc) % 2)

    def go(src, dst, device, send, recv):
        pltpu.make_async_remote_copy(
            src_ref=src,
            dst_ref=dst,
            send_sem=sends.at[send],
            recv_sem=recvs.at[recv],
            device_id=device,
            device_id_type=MESH,
        ).start()

    def got(recv, size):
        pltpu.make_async_copy(size, size, recvs.at[recv]).wait()

    def left(send, size):
        pltpu.make_async_copy(size, size, sends.at[send]).wait()

    img_peers = [(dx, dy) for dx in range(4) for dy in range(2) if dx or dy]
    cur_peers = [(dz, dy, dc) for dz in range(4) for dy in range(2) for dc in range(2) if dz or dy or dc]

    barrier = pltpu.get_barrier_semaphore()
    near = [img_dev(0, 1), img_dev(1, 0), img_dev(-1, 0)]
    near += [cur_dev(0, 1, 0), cur_dev(1, 0, 0), cur_dev(-1, 0, 0), cur_dev(0, 0, 1)]
    for d in near:
        pl.semaphore_signal(barrier, inc=1, device_id=d, device_id_type=MESH)
    pl.semaphore_wait(barrier, len(near))

    ring = ((1, 0), (-1, 1))
    back = ((1, 1), (-1, 0))
    G_Y, G_OWN, G_FAR, G_P, G_LAST, G_CORE = 0, 2, 6, 8, 10, 12

    def core(slot, h, group):
        go(C.at[slot, 0, HALF[h]], C.at[slot, 1, HALF[h]], cur_dev(0, 0, 1), 1, G_CORE + group)

    def both(i_src, c_src, slot, h, d, y, recv):
        go(i_src, I.at[slot, HALF[h]], img_dev(d, y), 0, recv)
        go(c_src, C.at[slot, 0, HALF[h]], cur_dev(d, y, 0), 0, recv)

    def onward(slot, to, h, d, y, recv):
        both(I.at[slot, HALF[h]], C.at[slot, 0, HALF[h]], to, h, d, y, recv)

    def own_sem(d, h):
        return G_OWN + (d + 1) + h

    for h in range(2):
        both(img_ref.at[HALF[h]], cur_ref.at[HALF[h]], 1, h, 0, 1, G_Y + h)
        for d, k in ring if h == 0 else back:
            both(img_ref.at[HALF[k]], cur_ref.at[HALF[k]], SLOT[-d, 0], k, d, 0, own_sem(d, k))
    go(cur_ref, C.at[0, 1], cur_dev(0, 0, 1), 1, G_CORE)
    I[0] = img_ref[...]
    C[0, 0] = cur_ref[...]
    pos = jnp.sum(img_ref[...].astype(F32) * cur_ref[...].astype(F32), axis=1, keepdims=True) * gain
    pos = jnp.sum(pos, axis=0, keepdims=True)
    for d, h in ring:
        got(own_sem(d, h), I.at[0])
        onward(SLOT[-d, 0], SLOT[2, 0], h, d, 0, G_FAR + h)
        core(SLOT[-d, 0], h, 0)
    for h in range(2):
        got(G_Y + h, I.at[0])
        for d, k in ring if h == 0 else back:
            onward(1, SLOT[-d, 1], h, d, 0, G_P + h)
        core(1, h, 0)
        if h == 0:
            for d, k in back:
                got(own_sem(d, k), I.at[0])
                core(SLOT[-d, 0], k, 0)

    def scores(rows, cols):
        r0, r1 = rows

        def step(q, carry):
            a = I[r0:r1].reshape((r1 - r0) * 128, 1024)
            s = nt(a, C[q].reshape(256, 1024)) * gain
            S[q, r0:r1] = s.reshape(r1 - r0, 128, 256)
            return carry

        lax.fori_loop(cols[0], cols[1], step, 0)

    def row_stats(rows, cols, fresh):
        def step(a, carry):
            parts = [S[q, a, :, h * 128 : h * 128 + 128] for q in range(*cols) for h in range(2)]
            m = functools.reduce(jnp.maximum, parts)
            if fresh:
                total = functools.reduce(jnp.add, [jnp.exp(v - m) for v in parts])
            else:
                old = RM[a]
                m = jnp.maximum(m, old)
                total = RL[a] * jnp.exp(old - m)
                total = functools.reduce(jnp.add, [jnp.exp(v - m) for v in parts], total)
            RM[a] = m
            RL[a] = total
            return carry

        lax.fori_loop(rows[0], rows[1], step, 0)

    def col_stats(rows, cols, fresh):
        r0, r1 = rows

        def step(q, carry):
            s = S[q, r0:r1].reshape((r1 - r0) * 16, 8, 256)
            m = jnp.max(s, axis=0)
            if not fresh:
                old = CM[q]
                m = jnp.maximum(m, old)
            total = jnp.sum(jnp.exp(s - m[None]), axis=0)
            if not fresh:
                total = total + CL[q] * jnp.exp(old - m)
            CM[q] = m
            CL[q] = total
            return carry

        lax.fori_loop(cols[0], cols[1], step, 0)

    got(G_CORE, S.at[0])
    scores((0, 4), (0, 4))
    for h in range(2):
        got(G_FAR + h, I.at[0])
        onward(SLOT[2, 0], SLOT[2, 1], h, 0, 1, G_LAST + h)
        core(SLOT[2, 0], h, 1)
    for h in range(2):
        got(G_P + h, I.at[0:2])
        core(SLOT[1, 1], h, 1)
        core(SLOT[-1, 1], h, 1)
    row_stats((0, 4), (0, 4), True)
    col_stats((0, 4), (0, 4), True)
    got(G_CORE + 1, S.at[0, 0:6])
    scores((4, 7), (0, 4))
    scores((0, 7), (4, 7))
    for h in range(2):
        got(G_LAST + h, I.at[0])
        core(SLOT[2, 1], h, 2)
    row_stats((0, 4), (4, 7), False)
    row_stats((4, 7), (0, 7), True)
    col_stats((4, 7), (0, 4), False)
    col_stats((0, 7), (4, 7), True)
    got(G_CORE + 2, I.at[0])
    scores((7, 8), (0, 7))
    scores((0, 8), (7, 8))
    row_stats((0, 7), (7, 8), False)
    row_stats((7, 8), (0, 8), True)
    col_stats((7, 8), (0, 7), False)
    col_stats((0, 8), (7, 8), True)

    def img_place(dx, dy):
        return ((x + dx + 4) % 4) * 2 + (yl + dy) % 2

    def cur_place(dz, dy, dc):
        return ((c + dc) % 2) * 8 + ((z + dz + 4) % 4) * 2 + (yh + dy) % 2

    mi = img_place(0, 0)
    mc = cur_place(0, 0, 0)
    for q, (dz, dy) in enumerate(PLACES):
        m = CM[q]
        high = jnp.max(m, axis=0, keepdims=True)
        lse = high + jnp.log(jnp.sum(CL[q] * jnp.exp(m - high), axis=0, keepdims=True))
        cst[mc, pl.ds(cur_place(dz, dy, 0), 1), :] = lse[:, :128]
        cst[mc, pl.ds(cur_place(dz, dy, 1), 1), :] = lse[:, 128:]
    for d in cur_peers:
        go(cst.at[mc], cst.at[mc], cur_dev(*d), 2, 15)
    for a, (dx, dy) in enumerate(PLACES):
        m = RM[a].T
        high = jnp.max(m, axis=0, keepdims=True)
        lse = high + jnp.log(jnp.sum(RL[a].T * jnp.exp(m - high), axis=0, keepdims=True))
        rst[mi, pl.ds(img_place(dx, dy), 1), :] = lse
    rst[mi, 8:16, :] = jnp.broadcast_to(pos, (8, 128))
    for d in img_peers:
        go(rst.at[mi], rst.at[mi], img_dev(*d), 3, 16)
    got(16, rst.at[0:7])
    parts = [rst[k, 0:8, :] for k in range(8)]
    high = functools.reduce(jnp.maximum, parts)
    tot_r[...] = high + jnp.log(functools.reduce(jnp.add, [jnp.exp(v - high) for v in parts]))
    for a, (dx, dy) in enumerate(PLACES):
        RM[a] = jnp.broadcast_to(tot_r[pl.ds(img_place(dx, dy), 1), :], (128, 128)).T
    got(15, cst.at[0:15])
    parts = [cst[k] for k in range(16)]
    high = functools.reduce(jnp.maximum, parts)
    tot_c[...] = high + jnp.log(functools.reduce(jnp.add, [jnp.exp(v - high) for v in parts]))

    for q, (dz, dy) in enumerate(PLACES):
        for h in range(2):
            CM[q, :, h * 128 : h * 128 + 128] = jnp.broadcast_to(tot_c[pl.ds(cur_place(dz, dy, h), 1), :], (8, 128))

    def weight_step(a, carry):
        rl = RM[a]
        for q in range(8):
            for h in range(2):
                lanes = slice(h * 128, h * 128 + 128)
                s = S[q, a, :, lanes]
                cl = CM[q, 0:1, lanes]
                W[q, a, :, lanes] = ((jnp.exp(s - rl) + jnp.exp(s - cl)) * 0.5).astype(BF16)
        return carry

    lax.fori_loop(0, 8, weight_step, 0)

    R_SWAP = 17

    def curve_part(q):
        part = tn(W[q].reshape(1024, 256), I[...].reshape(1024, 1024))
        qo[q, 1] = part[128:256]
        go(qo.at[q, 1], qoin.at[q], cur_dev(0, 0, 1), 4, R_SWAP + q)
        qo[q, 0] = part[0:128]

    def joined(q):
        got(R_SWAP + q, qoin.at[q])
        return qo[q, 0] + qoin[q]

    def image_part(a1, a2):
        w = jnp.concatenate(
            [jnp.concatenate([W[q, a] for q in range(8)], axis=1) for a in (a1, a2)], axis=0
        )
        return nn(w, C[...].reshape(2048, 1024))

    class Side:
        def __init__(self, w, into, keep, far, own, last, base, send, to):
            self.w, self.into, self.keep, self.far, self.own, self.last = w, into, keep, far, own, last
            self.base, self.send, self.to = base, send, to

        def go(self, y, k, h, d, dy, recv):
            go(self.w.at[y, k, h], self.into.at[y, k, h], self.to(d, dy), self.send, self.base + recv)

        def across(self, part):
            self.w[1, 0] = part.astype(BF16)
            for h in range(2):
                self.go(1, 0, HALF[h], 0, 1, h)

        def straight(self, d, part):
            k = 1 if d == 1 else 2
            self.w[1, k] = part.astype(BF16)
            self.go(1, k, slice(0, 128), d, 0, 2)

        def two_steps(self):
            for d, h in ring:
                got(self.base + h, py.at[0, HALF[0]])
                self.w[0, 0, HALF[h]] = (self.far[HALF[h]] + self.into[1, 0, HALF[h]].astype(F32)).astype(BF16)
                self.go(0, 0, HALF[h], d, 0, 3 + h)

        def first_half(self, d, part):
            k, through = (1, 0) if d == 1 else (2, 1)
            rest = HALF[1 - through]
            self.w[0, k, rest] = part[rest].astype(BF16)
            self.go(0, k, rest, d, 0, 5)
            self.keep[k - 1] = part[HALF[through]]

        def second_half(self):
            for d, h in ring:
                k = 1 if d == 1 else 2
                got(self.base + 3 + h, py.at[0, HALF[0]])
                self.w[0, k, HALF[h]] = (self.keep[k - 1] + self.into[0, 0, HALF[h]].astype(F32)).astype(BF16)
                self.go(0, k, HALF[h], d, 0, 5)

        def finish_partner(self):
            got(self.base + 2, I.at[0:2])
            self.last[0] = (self.own[1] + self.into[1, 1].astype(F32) + self.into[1, 2].astype(F32)).astype(BF16)
            go(self.last.at[0], self.last.at[1], self.to(0, 1), self.send, self.base + 6)

        def finish_own(self, other):
            got(self.base + 5, I.at[0:2])
            self.own[0] = self.own[0] + self.into[0, 1].astype(F32) + self.into[0, 2].astype(F32) - other

        def result(self):
            got(self.base + 6, I.at[0])
            return (self.own[0] + self.last[1].astype(F32)) * gain

    img = Side(pw, pin, pf, pa, pown, py, 25, 5, img_dev)
    cur = Side(qw, qin, qf, qa, qown, qy, 32, 5, lambda d, dy: cur_dev(d, dy, 0))

    curve_part(SLOT[2, 1])
    curve_part(SLOT[2, 0])
    part = image_part(SLOT[2, 1], SLOT[2, 0])
    img.across(part[0:128])
    pa[...] = part[128:256]
    cur.across(joined(SLOT[2, 1]))
    curve_part(SLOT[1, 1])
    curve_part(SLOT[-1, 1])
    part = image_part(SLOT[1, 1], SLOT[-1, 1])
    img.straight(1, part[0:128])
    img.straight(-1, part[128:256])
    cur.straight(1, joined(SLOT[1, 1]))
    cur.straight(-1, joined(SLOT[-1, 1]))
    qa[...] = joined(SLOT[2, 0])
    curve_part(SLOT[1, 0])
    curve_part(SLOT[-1, 0])
    img.two_steps()
    part = image_part(SLOT[1, 0], SLOT[-1, 0])
    cur.two_steps()
    img.first_half(1, part[0:128])
    img.first_half(-1, part[128:256])
    cur.first_half(1, joined(SLOT[1, 0]))
    cur.first_half(-1, joined(SLOT[-1, 0]))
    curve_part(SLOT[0, 1])
    curve_part(SLOT[0, 0])
    part = image_part(SLOT[0, 1], SLOT[0, 0])
    pown[1] = part[0:128]
    pown[0] = part[128:256]
    qown[1] = joined(SLOT[0, 1])
    qown[0] = joined(SLOT[0, 0])
    img.finish_partner()
    cur.finish_partner()
    img.second_half()
    cur.second_half()

    def grand(v):
        return jnp.sum(jnp.sum(v, axis=1, keepdims=True), axis=0, keepdims=True)

    pos_all = functools.reduce(jnp.add, [rst[k, 8:16, :] for k in range(8)])
    val_c[mc] = grand(tot_r[...]) - 2.0 * pos_all
    val_r[mi] = jnp.broadcast_to(grand(tot_c[...]), (8, 128))
    for d in cur_peers:
        go(val_c.at[mc], val_c.at[mc], cur_dev(*d), 6, 39)
    for d in img_peers:
        go(val_r.at[mi], val_r.at[mi], img_dev(*d), 7, 40)

    img.finish_own(cur_ref[...].astype(F32))
    cur.finish_own(img_ref[...].astype(F32))
    got(39, val_c.at[0:15])
    got(40, val_r.at[0:7])
    total = sum(val_c[k] for k in range(16)) + sum(val_r[k] for k in range(8))
    loss_ref[...] = total[0:1, 0:1] / (2.0 * pairs)
    dimg_ref[...] = img.result()
    dcur_ref[...] = cur.result()
    left(0, S.at[0:4, 0:7])
    left(1, S.at[0:2])
    left(2, cst.at[0:15])
    left(3, rst.at[0:7])
    left(4, S.at[0:4])
    left(5, S.at[0:4, 0:7])
    left(6, val_c.at[0:15])
    left(7, val_r.at[0:7])


def solution(mesh):
    def step(image_emb, curve_emb):
        gain = math.sqrt(image_emb.shape[1])
        vmem = pl.BlockSpec(memory_space=pltpu.VMEM)
        loss, dimg, dcur = pl.pallas_call(
            functools.partial(kernel, gain, 16384),
            out_shape=(
                jax.ShapeDtypeStruct((1, 1), F32),
                jax.ShapeDtypeStruct((128, 1024), F32),
                jax.ShapeDtypeStruct((128, 1024), F32),
            ),
            in_specs=[vmem, vmem],
            out_specs=(vmem, vmem, vmem),
            scratch_shapes=[
                pltpu.VMEM((8, 128, 1024), BF16),
                pltpu.VMEM((8, 2, 128, 1024), BF16),
                pltpu.VMEM((8, 8, 128, 256), F32),
                pltpu.VMEM((8, 8, 128, 256), BF16),
                pltpu.VMEM((8, 128, 128), F32),
                pltpu.VMEM((8, 128, 128), F32),
                pltpu.VMEM((8, 8, 256), F32),
                pltpu.VMEM((8, 8, 256), F32),
                pltpu.VMEM((8, 16, 128), F32),
                pltpu.VMEM((16, 16, 128), F32),
                pltpu.VMEM((8, 128), F32),
                pltpu.VMEM((16, 128), F32),
                pltpu.VMEM((8, 8, 128), F32),
                pltpu.VMEM((16, 8, 128), F32),
                pltpu.VMEM((2, 3, 128, 1024), BF16),
                pltpu.VMEM((2, 3, 128, 1024), BF16),
                pltpu.VMEM((2, 64, 1024), F32),
                pltpu.VMEM((128, 1024), F32),
                pltpu.VMEM((2, 128, 1024), F32),
                pltpu.VMEM((2, 128, 1024), BF16),
                pltpu.VMEM((8, 2, 128, 1024), F32),
                pltpu.VMEM((8, 128, 1024), F32),
                pltpu.VMEM((2, 3, 128, 1024), BF16),
                pltpu.VMEM((2, 3, 128, 1024), BF16),
                pltpu.VMEM((2, 64, 1024), F32),
                pltpu.VMEM((128, 1024), F32),
                pltpu.VMEM((2, 128, 1024), F32),
                pltpu.VMEM((2, 128, 1024), BF16),
                pltpu.SemaphoreType.DMA((8,)),
                pltpu.SemaphoreType.DMA((41,)),
            ],
            compiler_params=pltpu.CompilerParams(
                collective_id=0, has_side_effects=True, vmem_limit_bytes=48 << 20
            ),
        )(image_emb, curve_emb)
        return loss.reshape(()), dimg, dcur

    spec = P(("blk", "rep"), None)
    return jax.shard_map(step, mesh=mesh, in_specs=(spec, spec), out_specs=(P(), spec, spec), check_vma=False)
```

time: 80.6 us -> 75.5 us (0.937)
  Pallas kernels: 75.3 us -> 69.4 us
    pallas_call x1, Pallas kernels: 75.3 us -> 69.4 us  [step(): pl.pallas_call(functools.partial(kernel, gain, 16384), out_shape=(jax.Sha...]
    unnamed x4 -> x6, local copies, waits for them, and re-layouts: 2.74 us -> 3.48 us
where the time goes in v3:
time: 75.5 us; the launch traced here: 75.3 us
  Pallas kernels  69.4 us (92%)
  local copies, waits for them, and re-layouts  3.48 us (5%)
  between operations  2.41 us (3%)
    pallas_call x1, Pallas kernels, step(): pl.pallas_call(functools.partial(kernel, gain, 16384), out_shape=(jax.Sha...  69.4 us
    unnamed x6, local copies, waits for them, and re-layouts  3.48 us

profile of v3, /device:TPU:1, one launch (start us, length us, event | category | flops | bytes accessed | tf_op | source)
XLA Modules:
  0.0 75.3 jit_solution(7150145253429255434)
XLA Ops:
  0.6 0.0 copy-start
  0.6 0.9 %copy-done = bf16[128,1024]{1,0:T(8,128)(2,1)S(1)} copy-done((bf16[128,1024]{1,0:T(8,128)(2,1)S(1)}, bf16[128,1024]{1,0:T(8,128)(2,1)}, u32[]{:S(2)}) %copy-start) | copy-done | bytes 262168
  1.6 0.0 copy-start.1
  1.6 0.9 %copy-done.1 = bf16[128,1024]{1,0:T(8,128)(2,1)S(1)} copy-done((bf16[128,1024]{1,0:T(8,128)(2,1)S(1)}, bf16[128,1024]{1,0:T(8,128)(2,1)}, u32[]{:S(2)}) %copy-start.1) | copy-done | bytes 262168
  2.5 69.4 %shard_map.49 = (f32[1,1]{1,0:T(1,128)}, f32[128,1024]{1,0:T(8,128)S(1)}, f32[128,1024]{1,0:T(8,128)S(1)}) custom-call(bf16[128,1024]{1,0:T(8,128)(2,1)S(1)} %copy-done, bf16[128,1024]{1,0:T(8,128)(2,1)S(1)} %copy-done.1), custom_call_target="tpu_custom_call" | custom-call | tf_op jit(solution)/shard_map/pallas_call | solution.py:418
  72.6 0.8 %copy.9 = f32[128,1024]{1,0:T(8,128)} copy(f32[128,1024]{1,0:T(8,128)S(1)} %get-tuple-element.13) | data formatting | bytes 1048576
  73.4 0.8 %copy.10 = f32[128,1024]{1,0:T(8,128)} copy(f32[128,1024]{1,0:T(8,128)S(1)} %get-tuple-element.14) | data formatting | bytes 1048576
Async XLA Ops:
  0.6 1.0 %copy-start = (bf16[128,1024]{1,0:T(8,128)(2,1)S(1)}, bf16[128,1024]{1,0:T(8,128)(2,1)}, u32[]{:S(2)}) copy-start(bf16[128,1024]{1,0:T(8,128)(2,1)} %img_ref.1) | copy-start | bytes 786436
  1.6 0.9 %copy-start.1 = (bf16[128,1024]{1,0:T(8,128)(2,1)S(1)}, bf16[128,1024]{1,0:T(8,128)(2,1)}, u32[]{:S(2)}) copy-start(bf16[128,1024]{1,0:T(8,128)(2,1)} %cur_ref.1) | copy-start | bytes 786436

commit v4 on v3

--- a/solution.py
+++ b/solution.py
@@ -200,29 +200,29 @@
         got(G_FAR + h, I.at[0])
         onward(SLOT[2, 0], SLOT[2, 1], h, 0, 1, G_LAST + h)
         core(SLOT[2, 0], h, 1)
+    row_stats((0, 4), (0, 4), True)
+    col_stats((0, 4), (0, 4), True)
     for h in range(2):
         got(G_P + h, I.at[0:2])
         core(SLOT[1, 1], h, 1)
         core(SLOT[-1, 1], h, 1)
-    row_stats((0, 4), (0, 4), True)
-    col_stats((0, 4), (0, 4), True)
     got(G_CORE + 1, S.at[0, 0:6])
     scores((4, 7), (0, 4))
     scores((0, 7), (4, 7))
-    for h in range(2):
-        got(G_LAST + h, I.at[0])
-        core(SLOT[2, 1], h, 2)
     row_stats((0, 4), (4, 7), False)
     row_stats((4, 7), (0, 7), True)
     col_stats((4, 7), (0, 4), False)
     col_stats((0, 7), (4, 7), True)
+    for h in range(2):
+        got(G_LAST + h, I.at[0])
+        core(SLOT[2, 1], h, 2)
+    scores((7, 8), (0, 7))
     got(G_CORE + 2, I.at[0])
-    scores((7, 8), (0, 7))
     scores((0, 8), (7, 8))
+    col_stats((7, 8), (0, 7), False)
+    col_stats((0, 8), (7, 8), True)
     row_stats((0, 7), (7, 8), False)
     row_stats((7, 8), (0, 8), True)
-    col_stats((7, 8), (0, 7), False)
-    col_stats((0, 8), (7, 8), True)
 
     def img_place(dx, dy):
         return ((x + dx + 4) % 4) * 2 + (yl + dy) % 2
@@ -263,17 +263,29 @@
         for h in range(2):
             CM[q, :, h * 128 : h * 128 + 128] = jnp.broadcast_to(tot_c[pl.ds(cur_place(dz, dy, h), 1), :], (8, 128))
 
-    def weight_step(a, carry):
+    def weigh(q, a):
         rl = RM[a]
-        for q in range(8):
-            for h in range(2):
-                lanes = slice(h * 128, h * 128 + 128)
-                s = S[q, a, :, lanes]
-                cl = CM[q, 0:1, lanes]
-                W[q, a, :, lanes] = ((jnp.exp(s - rl) + jnp.exp(s - cl)) * 0.5).astype(BF16)
-        return carry
-
-    lax.fori_loop(0, 8, weight_step, 0)
+        for h in range(2):
+            lanes = slice(h * 128, h * 128 + 128)
+            s = S[q, a, :, lanes]
+            cl = CM[q, 0:1, lanes]
+            W[q, a, :, lanes] = ((jnp.exp(s - rl) + jnp.exp(s - cl)) * 0.5).astype(BF16)
+
+    def weights_by_row(rows, qs):
+        def step(a, carry):
+            for q in qs:
+                weigh(q, a)
+            return carry
+
+        lax.fori_loop(rows[0], rows[1], step, 0)
+
+    def weights_by_col(cols, rows):
+        def step(q, carry):
+            for a in rows:
+                weigh(q, a)
+            return carry
+
+        lax.fori_loop(cols[0], cols[1], step, 0)
 
     R_SWAP = 17
 
@@ -347,24 +359,30 @@
     img = Side(pw, pin, pf, pa, pown, py, 25, 5, img_dev)
     cur = Side(qw, qin, qf, qa, qown, qy, 32, 5, lambda d, dy: cur_dev(d, dy, 0))
 
+    weights_by_row((0, 8), (7,))
     curve_part(SLOT[2, 1])
-    curve_part(SLOT[2, 0])
+    weights_by_col((0, 7), (4, 7))
     part = image_part(SLOT[2, 1], SLOT[2, 0])
     img.across(part[0:128])
     pa[...] = part[128:256]
     cur.across(joined(SLOT[2, 1]))
+    weights_by_row((0, 4), (5, 6))
+    weights_by_row((5, 7), (5, 6))
     curve_part(SLOT[1, 1])
     curve_part(SLOT[-1, 1])
+    weights_by_col((0, 5), (5, 6))
     part = image_part(SLOT[1, 1], SLOT[-1, 1])
     img.straight(1, part[0:128])
     img.straight(-1, part[128:256])
     cur.straight(1, joined(SLOT[1, 1]))
     cur.straight(-1, joined(SLOT[-1, 1]))
-    qa[...] = joined(SLOT[2, 0])
+    weights_by_col((0, 5), (0, 1, 2, 3))
+    curve_part(SLOT[2, 0])
     curve_part(SLOT[1, 0])
     curve_part(SLOT[-1, 0])
+    part = image_part(SLOT[1, 0], SLOT[-1, 0])
     img.two_steps()
-    part = image_part(SLOT[1, 0], SLOT[-1, 0])
+    qa[...] = joined(SLOT[2, 0])
     cur.two_steps()
     img.first_half(1, part[0:128])
     img.first_half(-1, part[128:256])

time: 75.5 us -> 72.8 us (0.964)
  Pallas kernels: 69.4 us -> 66.7 us
    pallas_call x1, Pallas kernels: 69.4 us -> 66.7 us  [step(): pl.pallas_call(functools.partial(kernel, gain, 16384), out_shape=(jax.Sha...]
where the time goes in v4:
time: 72.8 us; the launch traced here: 72.6 us
  Pallas kernels  66.7 us (92%)
  local copies, waits for them, and re-layouts  3.48 us (5%)
  between operations  2.41 us (3%)
    pallas_call x1, Pallas kernels, step(): pl.pallas_call(functools.partial(kernel, gain, 16384), out_shape=(jax.Sha...  66.7 us
    unnamed x6, local copies, waits for them, and re-layouts  3.48 us

profile of v4, /device:TPU:1, one launch (start us, length us, event | category | flops | bytes accessed | tf_op | source)
XLA Modules:
  0.0 72.6 jit_solution(16652444308429579889)
XLA Ops:
  0.6 0.0 copy-start
  0.6 0.9 %copy-done = bf16[128,1024]{1,0:T(8,128)(2,1)S(1)} copy-done((bf16[128,1024]{1,0:T(8,128)(2,1)S(1)}, bf16[128,1024]{1,0:T(8,128)(2,1)}, u32[]{:S(2)}) %copy-start) | copy-done | bytes 262168
  1.6 0.0 copy-start.1
  1.6 0.9 %copy-done.1 = bf16[128,1024]{1,0:T(8,128)(2,1)S(1)} copy-done((bf16[128,1024]{1,0:T(8,128)(2,1)S(1)}, bf16[128,1024]{1,0:T(8,128)(2,1)}, u32[]{:S(2)}) %copy-start.1) | copy-done | bytes 262168
  2.5 66.7 %shard_map.49 = (f32[1,1]{1,0:T(1,128)}, f32[128,1024]{1,0:T(8,128)S(1)}, f32[128,1024]{1,0:T(8,128)S(1)}) custom-call(bf16[128,1024]{1,0:T(8,128)(2,1)S(1)} %copy-done, bf16[128,1024]{1,0:T(8,128)(2,1)S(1)} %copy-done.1), custom_call_target="tpu_custom_call" | custom-call | tf_op jit(solution)/shard_map/pallas_call | solution.py:436
  69.9 0.8 %copy.9 = f32[128,1024]{1,0:T(8,128)} copy(f32[128,1024]{1,0:T(8,128)S(1)} %get-tuple-element.13) | data formatting | bytes 1048576
  70.7 0.8 %copy.10 = f32[128,1024]{1,0:T(8,128)} copy(f32[128,1024]{1,0:T(8,128)S(1)} %get-tuple-element.14) | data formatting | bytes 1048576
Async XLA Ops:
  0.6 1.0 %copy-start = (bf16[128,1024]{1,0:T(8,128)(2,1)S(1)}, bf16[128,1024]{1,0:T(8,128)(2,1)}, u32[]{:S(2)}) copy-start(bf16[128,1024]{1,0:T(8,128)(2,1)} %img_ref.1) | copy-start | bytes 786436
  1.6 0.9 %copy-start.1 = (bf16[128,1024]{1,0:T(8,128)(2,1)S(1)}, bf16[128,1024]{1,0:T(8,128)(2,1)}, u32[]{:S(2)}) copy-start(bf16[128,1024]{1,0:T(8,128)(2,1)} %cur_ref.1) | copy-start | bytes 786436

commit v5 on v4

--- a/solution.py
+++ b/solution.py
@@ -65,6 +65,7 @@
     qy,
     sends,
     recvs,
+    locals_,
 ):
     blk, rep = lax.axis_index("blk"), lax.axis_index("rep")
     x = blk % 4
@@ -98,6 +99,11 @@
     def left(send, size):
         pltpu.make_async_copy(size, size, sends.at[send]).wait()
 
+    load_i = pltpu.make_async_copy(img_ref, I.at[0], locals_.at[0])
+    load_c = pltpu.make_async_copy(cur_ref, C.at[0, 0], locals_.at[1])
+    load_i.start()
+    load_c.start()
+
     img_peers = [(dx, dy) for dx in range(4) for dy in range(2) if dx or dy]
     cur_peers = [(dz, dy, dc) for dz in range(4) for dy in range(2) for dc in range(2) if dz or dy or dc]
 
@@ -106,6 +112,8 @@
     near += [cur_dev(0, 1, 0), cur_dev(1, 0, 0), cur_dev(-1, 0, 0), cur_dev(0, 0, 1)]
     for d in near:
         pl.semaphore_signal(barrier, inc=1, device_id=d, device_id_type=MESH)
+    load_i.wait()
+    load_c.wait()
     pl.semaphore_wait(barrier, len(near))
 
     ring = ((1, 0), (-1, 1))
@@ -126,13 +134,11 @@
         return G_OWN + (d + 1) + h
 
     for h in range(2):
-        both(img_ref.at[HALF[h]], cur_ref.at[HALF[h]], 1, h, 0, 1, G_Y + h)
+        both(I.at[0, HALF[h]], C.at[0, 0, HALF[h]], 1, h, 0, 1, G_Y + h)
         for d, k in ring if h == 0 else back:
-            both(img_ref.at[HALF[k]], cur_ref.at[HALF[k]], SLOT[-d, 0], k, d, 0, own_sem(d, k))
-    go(cur_ref, C.at[0, 1], cur_dev(0, 0, 1), 1, G_CORE)
-    I[0] = img_ref[...]
-    C[0, 0] = cur_ref[...]
-    pos = jnp.sum(img_ref[...].astype(F32) * cur_ref[...].astype(F32), axis=1, keepdims=True) * gain
+            both(I.at[0, HALF[k]], C.at[0, 0, HALF[k]], SLOT[-d, 0], k, d, 0, own_sem(d, k))
+    go(C.at[0, 0], C.at[0, 1], cur_dev(0, 0, 1), 1, G_CORE)
+    pos = jnp.sum(I[0].astype(F32) * C[0, 0].astype(F32), axis=1, keepdims=True) * gain
     pos = jnp.sum(pos, axis=0, keepdims=True)
     for d, h in ring:
         got(own_sem(d, h), I.at[0])
@@ -151,13 +157,14 @@
     def scores(rows, cols):
         r0, r1 = rows
 
-        def step(q, carry):
+        def some(q, n):
             a = I[r0:r1].reshape((r1 - r0) * 128, 1024)
-            s = nt(a, C[q].reshape(256, 1024)) * gain
-            S[q, r0:r1] = s.reshape(r1 - r0, 128, 256)
-            return carry
-
-        lax.fori_loop(cols[0], cols[1], step, 0)
+            s = nt(a, C[pl.ds(q, n)].reshape(n * 256, 1024)) * gain
+            for k in range(n):
+                S[q + k, r0:r1] = s[:, k * 256 : k * 256 + 256].reshape(r1 - r0, 128, 256)
+
+        for q in range(cols[0], cols[1], 4):
+            some(q, min(4, cols[1] - q))
 
     def row_stats(rows, cols, fresh):
         def step(a, carry):
@@ -202,22 +209,25 @@
         core(SLOT[2, 0], h, 1)
     row_stats((0, 4), (0, 4), True)
     col_stats((0, 4), (0, 4), True)
+    got(G_CORE + 1, I.at[0])
+    scores((4, 5), (0, 4))
+    scores((0, 5), (4, 5))
     for h in range(2):
         got(G_P + h, I.at[0:2])
-        core(SLOT[1, 1], h, 1)
-        core(SLOT[-1, 1], h, 1)
-    got(G_CORE + 1, S.at[0, 0:6])
-    scores((4, 7), (0, 4))
-    scores((0, 7), (4, 7))
+        core(SLOT[1, 1], h, 2)
+        core(SLOT[-1, 1], h, 2)
+    got(G_CORE + 2, I.at[0:2])
+    scores((5, 7), (0, 5))
+    scores((0, 7), (5, 7))
     row_stats((0, 4), (4, 7), False)
     row_stats((4, 7), (0, 7), True)
     col_stats((4, 7), (0, 4), False)
     col_stats((0, 7), (4, 7), True)
     for h in range(2):
         got(G_LAST + h, I.at[0])
-        core(SLOT[2, 1], h, 2)
+        core(SLOT[2, 1], h, 3)
     scores((7, 8), (0, 7))
-    got(G_CORE + 2, I.at[0])
+    got(G_CORE + 3, I.at[0])
     scores((0, 8), (7, 8))
     col_stats((7, 8), (0, 7), False)
     col_stats((0, 8), (7, 8), True)
@@ -239,7 +249,7 @@
         cst[mc, pl.ds(cur_place(dz, dy, 0), 1), :] = lse[:, :128]
         cst[mc, pl.ds(cur_place(dz, dy, 1), 1), :] = lse[:, 128:]
     for d in cur_peers:
-        go(cst.at[mc], cst.at[mc], cur_dev(*d), 2, 15)
+        go(cst.at[mc], cst.at[mc], cur_dev(*d), 2, 16)
     for a, (dx, dy) in enumerate(PLACES):
         m = RM[a].T
         high = jnp.max(m, axis=0, keepdims=True)
@@ -247,14 +257,14 @@
         rst[mi, pl.ds(img_place(dx, dy), 1), :] = lse
     rst[mi, 8:16, :] = jnp.broadcast_to(pos, (8, 128))
     for d in img_peers:
-        go(rst.at[mi], rst.at[mi], img_dev(*d), 3, 16)
-    got(16, rst.at[0:7])
+        go(rst.at[mi], rst.at[mi], img_dev(*d), 3, 17)
+    got(17, rst.at[0:7])
     parts = [rst[k, 0:8, :] for k in range(8)]
     high = functools.reduce(jnp.maximum, parts)
     tot_r[...] = high + jnp.log(functools.reduce(jnp.add, [jnp.exp(v - high) for v in parts]))
     for a, (dx, dy) in enumerate(PLACES):
         RM[a] = jnp.broadcast_to(tot_r[pl.ds(img_place(dx, dy), 1), :], (128, 128)).T
-    got(15, cst.at[0:15])
+    got(16, cst.at[0:15])
     parts = [cst[k] for k in range(16)]
     high = functools.reduce(jnp.maximum, parts)
     tot_c[...] = high + jnp.log(functools.reduce(jnp.add, [jnp.exp(v - high) for v in parts]))
@@ -287,7 +297,7 @@
 
         lax.fori_loop(cols[0], cols[1], step, 0)
 
-    R_SWAP = 17
+    R_SWAP = 18
 
     def curve_part(q):
         part = tn(W[q].reshape(1024, 256), I[...].reshape(1024, 1024))
@@ -356,8 +366,8 @@
             got(self.base + 6, I.at[0])
             return (self.own[0] + self.last[1].astype(F32)) * gain
 
-    img = Side(pw, pin, pf, pa, pown, py, 25, 5, img_dev)
-    cur = Side(qw, qin, qf, qa, qown, qy, 32, 5, lambda d, dy: cur_dev(d, dy, 0))
+    img = Side(pw, pin, pf, pa, pown, py, 26, 5, img_dev)
+    cur = Side(qw, qin, qf, qa, qown, qy, 33, 5, lambda d, dy: cur_dev(d, dy, 0))
 
     weights_by_row((0, 8), (7,))
     curve_part(SLOT[2, 1])
@@ -407,14 +417,14 @@
     val_c[mc] = grand(tot_r[...]) - 2.0 * pos_all
     val_r[mi] = jnp.broadcast_to(grand(tot_c[...]), (8, 128))
     for d in cur_peers:
-        go(val_c.at[mc], val_c.at[mc], cur_dev(*d), 6, 39)
+        go(val_c.at[mc], val_c.at[mc], cur_dev(*d), 6, 40)
     for d in img_peers:
-        go(val_r.at[mi], val_r.at[mi], img_dev(*d), 7, 40)
-
-    img.finish_own(cur_ref[...].astype(F32))
-    cur.finish_own(img_ref[...].astype(F32))
-    got(39, val_c.at[0:15])
-    got(40, val_r.at[0:7])
+        go(val_r.at[mi], val_r.at[mi], img_dev(*d), 7, 41)
+
+    img.finish_own(C[0, 0].astype(F32))
+    cur.finish_own(I[0].astype(F32))
+    got(40, val_c.at[0:15])
+    got(41, val_r.at[0:7])
     total = sum(val_c[k] for k in range(16)) + sum(val_r[k] for k in range(8))
     loss_ref[...] = total[0:1, 0:1] / (2.0 * pairs)
     dimg_ref[...] = img.result()
@@ -440,7 +450,7 @@
                 jax.ShapeDtypeStruct((128, 1024), F32),
                 jax.ShapeDtypeStruct((128, 1024), F32),
             ),
-            in_specs=[vmem, vmem],
+            in_specs=[pl.BlockSpec(memory_space=pltpu.HBM)] * 2,
             out_specs=(vmem, vmem, vmem),
             scratch_shapes=[
                 pltpu.VMEM((8, 128, 1024), BF16),
@@ -472,10 +482,11 @@
                 pltpu.VMEM((2, 128, 1024), F32),
                 pltpu.VMEM((2, 128, 1024), BF16),
                 pltpu.SemaphoreType.DMA((8,)),
-                pltpu.SemaphoreType.DMA((41,)),
+                pltpu.SemaphoreType.DMA((42,)),
+                pltpu.SemaphoreType.DMA((2,)),
             ],
             compiler_params=pltpu.CompilerParams(
-                collective_id=0, has_side_effects=True, vmem_limit_bytes=48 << 20
+                collective_id=0, has_side_effects=True, vmem_limit_bytes=57 << 20
             ),
         )(image_emb, curve_emb)
         return loss.reshape(()), dimg, dcur

time: 72.8 us -> 70.9 us (0.974)
  Pallas kernels: 66.7 us -> 65.6 us
  local copies, waits for them, and re-layouts: 3.48 us -> 2.74 us
    pallas_call x1, Pallas kernels: 66.7 us -> 65.6 us  [step(): pl.pallas_call(functools.partial(kernel, gain, 16384), out_shape=(jax.Sha...]
    unnamed x6 -> x4, local copies, waits for them, and re-layouts: 3.48 us -> 2.74 us
where the time goes in v5:
time: 70.9 us; the launch traced here: 70.7 us
  Pallas kernels  65.6 us (93%)
  local copies, waits for them, and re-layouts  2.74 us (4%)
  between operations  2.41 us (3%)
    pallas_call x1, Pallas kernels, step(): pl.pallas_call(functools.partial(kernel, gain, 16384), out_shape=(jax.Sha...  65.6 us
    unnamed x4, local copies, waits for them, and re-layouts  2.74 us

profile of v5, /device:TPU:1, one launch (start us, length us, event | category | flops | bytes accessed | tf_op | source)
XLA Modules:
  0.0 70.7 jit_solution(2848414743829549550)
XLA Ops:
  0.6 65.6 %shard_map.49 = (f32[1,1]{1,0:T(1,128)}, f32[128,1024]{1,0:T(8,128)}, f32[128,1024]{1,0:T(8,128)}) custom-call(bf16[128,1024]{1,0:T(8,128)(2,1)} %img_ref.1, bf16[128,1024]{1,0:T(8,128)(2,1)} %cur_ref.1), custom_call_target="tpu_custom_call" | custom-call | tf_op jit(solution)/shard_map/pallas_call | solution.py:446
  66.9 0.0 copy-start
  66.9 1.9 %copy.9 = f32[128,1024]{1,0:T(8,128)} copy(f32[128,1024]{1,0:T(8,128)} %get-tuple-element.13) | data formatting | bytes 1048576
  68.8 0.0 copy-done
  68.8 0.8 %copy.10 = f32[128,1024]{1,0:T(8,128)} copy(f32[128,1024]{1,0:T(8,128)S(1)} %copy-done) | data formatting | bytes 1048576
Async XLA Ops:
  66.9 2.0 %copy-start = (f32[128,1024]{1,0:T(8,128)S(1)}, f32[128,1024]{1,0:T(8,128)}, u32[]{:S(2)}) copy-start(f32[128,1024]{1,0:T(8,128)} %get-tuple-element.14) | copy-start | bytes 1572868

commit v6 on v5

--- a/solution.py
+++ b/solution.py
@@ -201,12 +201,12 @@
 
         lax.fori_loop(cols[0], cols[1], step, 0)
 
-    got(G_CORE, S.at[0])
-    scores((0, 4), (0, 4))
     for h in range(2):
         got(G_FAR + h, I.at[0])
         onward(SLOT[2, 0], SLOT[2, 1], h, 0, 1, G_LAST + h)
         core(SLOT[2, 0], h, 1)
+    got(G_CORE, S.at[0])
+    scores((0, 4), (0, 4))
     row_stats((0, 4), (0, 4), True)
     col_stats((0, 4), (0, 4), True)
     got(G_CORE + 1, I.at[0])
@@ -386,6 +386,17 @@
     img.straight(-1, part[128:256])
     cur.straight(1, joined(SLOT[1, 1]))
     cur.straight(-1, joined(SLOT[-1, 1]))
+    def grand(v):
+        return jnp.sum(jnp.sum(v, axis=1, keepdims=True), axis=0, keepdims=True)
+
+    pos_all = functools.reduce(jnp.add, [rst[k, 8:16, :] for k in range(8)])
+    val_c[mc] = grand(tot_r[...]) - 2.0 * pos_all
+    val_r[mi] = jnp.broadcast_to(grand(tot_c[...]), (8, 128))
+    for d in cur_peers:
+        go(val_c.at[mc], val_c.at[mc], cur_dev(*d), 6, 40)
+    for d in img_peers:
+        go(val_r.at[mi], val_r.at[mi], img_dev(*d), 7, 41)
+
     weights_by_col((0, 5), (0, 1, 2, 3))
     curve_part(SLOT[2, 0])
     curve_part(SLOT[1, 0])
@@ -409,17 +420,6 @@
     cur.finish_partner()
     img.second_half()
     cur.second_half()
-
-    def grand(v):
-        return jnp.sum(jnp.sum(v, axis=1, keepdims=True), axis=0, keepdims=True)
-
-    pos_all = functools.reduce(jnp.add, [rst[k, 8:16, :] for k in range(8)])
-    val_c[mc] = grand(tot_r[...]) - 2.0 * pos_all
-    val_r[mi] = jnp.broadcast_to(grand(tot_c[...]), (8, 128))
-    for d in cur_peers:
-        go(val_c.at[mc], val_c.at[mc], cur_dev(*d), 6, 40)
-    for d in img_peers:
-        go(val_r.at[mi], val_r.at[mi], img_dev(*d), 7, 41)
 
     img.finish_own(C[0, 0].astype(F32))
     cur.finish_own(I[0].astype(F32))

time: 70.9 us -> 69.8 us (0.984)
  Pallas kernels: 65.6 us -> 64.5 us
    pallas_call x1, Pallas kernels: 65.6 us -> 64.5 us  [step(): pl.pallas_call(functools.partial(kernel, gain, 16384), out_shape=(jax.Sha...]
where the time goes in v6:
time: 69.8 us; the launch traced here: 69.7 us
  Pallas kernels  64.5 us (92%)
  local copies, waits for them, and re-layouts  2.74 us (4%)
  between operations  2.41 us (3%)
    pallas_call x1, Pallas kernels, step(): pl.pallas_call(functools.partial(kernel, gain, 16384), out_shape=(jax.Sha...  64.5 us
    unnamed x4, local copies, waits for them, and re-layouts  2.74 us

profile of v6, /device:TPU:1, one launch (start us, length us, event | category | flops | bytes accessed | tf_op | source)
XLA Modules:
  0.0 69.7 jit_solution(5296127633783634813)
XLA Ops:
  0.6 64.5 %shard_map.49 = (f32[1,1]{1,0:T(1,128)}, f32[128,1024]{1,0:T(8,128)}, f32[128,1024]{1,0:T(8,128)}) custom-call(bf16[128,1024]{1,0:T(8,128)(2,1)} %img_ref.1, bf16[128,1024]{1,0:T(8,128)(2,1)} %cur_ref.1), custom_call_target="tpu_custom_call" | custom-call | tf_op jit(solution)/shard_map/pallas_call | solution.py:446
  65.8 0.0 copy-start
  65.8 1.9 %copy.9 = f32[128,1024]{1,0:T(8,128)} copy(f32[128,1024]{1,0:T(8,128)} %get-tuple-element.13) | data formatting | bytes 1048576
  67.7 0.0 copy-done
  67.7 0.8 %copy.10 = f32[128,1024]{1,0:T(8,128)} copy(f32[128,1024]{1,0:T(8,128)S(1)} %copy-done) | data formatting | bytes 1048576
Async XLA Ops:
  65.8 2.0 %copy-start = (f32[128,1024]{1,0:T(8,128)S(1)}, f32[128,1024]{1,0:T(8,128)}, u32[]{:S(2)}) copy-start(f32[128,1024]{1,0:T(8,128)} %get-tuple-element.14) | copy-start | bytes 1572868

commit v7 on v6

--- a/solution.py
+++ b/solution.py
@@ -263,7 +263,7 @@
     high = functools.reduce(jnp.maximum, parts)
     tot_r[...] = high + jnp.log(functools.reduce(jnp.add, [jnp.exp(v - high) for v in parts]))
     for a, (dx, dy) in enumerate(PLACES):
-        RM[a] = jnp.broadcast_to(tot_r[pl.ds(img_place(dx, dy), 1), :], (128, 128)).T
+        RM[a] = jnp.broadcast_to(tot_r[pl.ds(img_place(dx, dy), 1), :] + math.log(2.0), (128, 128)).T
     got(16, cst.at[0:15])
     parts = [cst[k] for k in range(16)]
     high = functools.reduce(jnp.maximum, parts)
@@ -271,7 +271,7 @@
 
     for q, (dz, dy) in enumerate(PLACES):
         for h in range(2):
-            CM[q, :, h * 128 : h * 128 + 128] = jnp.broadcast_to(tot_c[pl.ds(cur_place(dz, dy, h), 1), :], (8, 128))
+            CM[q, :, h * 128 : h * 128 + 128] = jnp.broadcast_to(tot_c[pl.ds(cur_place(dz, dy, h), 1), :] + math.log(2.0), (8, 128))
 
     def weigh(q, a):
         rl = RM[a]
@@ -279,7 +279,7 @@
             lanes = slice(h * 128, h * 128 + 128)
             s = S[q, a, :, lanes]
             cl = CM[q, 0:1, lanes]
-            W[q, a, :, lanes] = ((jnp.exp(s - rl) + jnp.exp(s - cl)) * 0.5).astype(BF16)
+            W[q, a, :, lanes] = (jnp.exp(s - rl) + jnp.exp(s - cl)).astype(BF16)
 
     def weights_by_row(rows, qs):
         def step(a, carry):

time: 69.8 us -> 69.7 us (level)
  no operation moved by 1% of the time
where the time goes in v7:
time: 69.7 us; the launch traced here: 69.5 us
  Pallas kernels  64.3 us (92%)
  local copies, waits for them, and re-layouts  2.74 us (4%)
  between operations  2.41 us (3%)
    pallas_call x1, Pallas kernels, step(): pl.pallas_call(functools.partial(kernel, gain, 16384), out_shape=(jax.Sha...  64.3 us
    unnamed x4, local copies, waits for them, and re-layouts  2.74 us

profile of v7, /device:TPU:1, one launch (start us, length us, event | category | flops | bytes accessed | tf_op | source)
XLA Modules:
  0.0 69.5 jit_solution(628551068948732146)
XLA Ops:
  0.6 64.3 %shard_map.49 = (f32[1,1]{1,0:T(1,128)}, f32[128,1024]{1,0:T(8,128)}, f32[128,1024]{1,0:T(8,128)}) custom-call(bf16[128,1024]{1,0:T(8,128)(2,1)} %img_ref.1, bf16[128,1024]{1,0:T(8,128)(2,1)} %cur_ref.1), custom_call_target="tpu_custom_call" | custom-call | tf_op jit(solution)/shard_map/pallas_call | solution.py:446
  65.6 0.0 copy-start
  65.6 1.9 %copy.9 = f32[128,1024]{1,0:T(8,128)} copy(f32[128,1024]{1,0:T(8,128)} %get-tuple-element.13) | data formatting | bytes 1048576
  67.6 0.0 copy-done
  67.6 0.8 %copy.10 = f32[128,1024]{1,0:T(8,128)} copy(f32[128,1024]{1,0:T(8,128)S(1)} %copy-done) | data formatting | bytes 1048576
Async XLA Ops:
  65.6 2.0 %copy-start = (f32[128,1024]{1,0:T(8,128)S(1)}, f32[128,1024]{1,0:T(8,128)}, u32[]{:S(2)}) copy-start(f32[128,1024]{1,0:T(8,128)} %get-tuple-element.14) | copy-start | bytes 1572868
